TPU v7x, 128 devices: a whole 4x4x4 slice. The times are simulated.
128 devices in a mesh: row: 64 (over z, y, x), col: 2 (over core).
Axes of the slice: x: 4, y: 4, z: 4, core: 2. Of those that a mesh axis runs over, the one named last changes fastest.
Arguments:
- slab: bfloat16 [262144, 2048], P('row', 'col'), may hold values from -6 to 6
- gauss: bfloat16 [2048, 1024], P('col'), may hold values from -0.125 to 0.125
- pivots: int32 [1024], replicated, may hold values from 0 to 262143, as said below
- block_inverses: float32 [8, 128, 128], replicated, may hold values from -2 to 2
Outputs:
- factor_rows: float32 [262144, 1024], P(('row', 'col'))
- pivot_block: float32 [1024, 1024], P(('row', 'col'))
Inputs may be any that keep to these rules, and one draw needn't show every extreme that they name: `pivots`: distinct row numbers; each aligned block of 2048 rows holds at most 32 of them, and some block holds exactly 32.
All inputs are finite; a program needn't handle non-finite values.
Results may differ from a plain program's by a relative error of at most 0.0003.
Values may be sent and summed in bfloat16 or wider, within the bound.
A program may use at most 128 MiB of HBM per device.

v0:
```python
import functools

import jax
import jax.numpy as jnp
from jax import lax
from jax.experimental import pallas as pl
from jax.experimental.pallas import tpu as pltpu
from jax.sharding import PartitionSpec as P

K = 1024
BLK = 128
SLOTS = 32
TM = 1024


def split(x):
    hi = x.astype(jnp.bfloat16)
    return hi, (x - hi.astype(jnp.float32)).astype(jnp.bfloat16)


def solve_kernel(factor, s_ref, p_ref, b_ref, f_ref, pcat, bcat, g):
    nb = s_ref.shape[1] // BLK

    @pl.when(pl.program_id(0) == 0)
    def _():
        for i in range(nb):
            hi, lo = split(p_ref[i * BLK:(i + 1) * BLK, :] * factor)
            pcat[3 * i * BLK:(3 * i + 1) * BLK, :] = hi
            pcat[(3 * i + 1) * BLK:(3 * i + 2) * BLK, :] = lo
            pcat[(3 * i + 2) * BLK:(3 * i + 3) * BLK, :] = hi
            bh, bl = split(b_ref[i])
            bcat[i, 0:BLK, :] = bh
            bcat[i, BLK:2 * BLK, :] = bl
            bcat[i, 2 * BLK:3 * BLK, :] = bh
    for j in range(nb):
        cols = slice(j * BLK, (j + 1) * BLK)
        acc = s_ref[:, cols]
        if j > 0:
            acc = acc - jnp.dot(g[:, : 3 * j * BLK], pcat[: 3 * j * BLK, cols], preferred_element_type=jnp.float32)
        a_hi, a_lo = split(acc)
        out = jnp.dot(jnp.concatenate([a_hi, a_hi, a_lo], axis=1), bcat[j], preferred_element_type=jnp.float32)
        f_ref[:, cols] = out
        if j + 1 < nb:
            o_hi, o_lo = split(out)
            g[:, 3 * j * BLK:(3 * j + 1) * BLK] = o_hi
            g[:, (3 * j + 1) * BLK:(3 * j + 2) * BLK] = o_hi
            g[:, (3 * j + 2) * BLK:(3 * j + 3) * BLK] = o_lo


def solve(sketch, pivot_block, block_inverses):
    rows, k = sketch.shape
    nb = k // BLK
    full = lambda shape: pl.BlockSpec(shape, lambda i: (0,) * len(shape))
    return pl.pallas_call(
        functools.partial(solve_kernel, 1.0 / k**0.5),
        out_shape=jax.ShapeDtypeStruct((rows, k), jnp.float32),
        grid=(rows // TM,),
        in_specs=[pl.BlockSpec((TM, k), lambda i: (i, 0)), full((k, k)), full(block_inverses.shape)],
        out_specs=pl.BlockSpec((TM, k), lambda i: (i, 0)),
        scratch_shapes=[pltpu.VMEM((3 * k, k), jnp.bfloat16), pltpu.VMEM((nb, 3 * BLK, BLK), jnp.bfloat16), pltpu.VMEM((TM, 3 * k), jnp.bfloat16)],
        compiler_params=pltpu.CompilerParams(vmem_limit_bytes=48 * 1024 * 1024),
    )(sketch, pivot_block, block_inverses)


def on_device(slab, gauss, pivots, block_inverses):
    col_count = lax.axis_size("col")
    devices = lax.axis_size("row") * col_count
    col = lax.axis_index("col")
    owner = lax.axis_index("row") * col_count + col
    shard_rows = slab.shape[0] // col_count
    width = gauss.shape[1]
    swap = [(0, 1), (1, 0)]

    order = jnp.arange(pivots.shape[0], dtype=jnp.int32)
    block_of = pivots // shard_rows
    same = (block_of[:, None] == block_of[None, :]) & (order[None, :] < order[:, None])
    rank = jnp.sum(same.astype(jnp.int32), axis=1)
    local = pivots - block_of * shard_rows
    partner = owner + 1 - 2 * col
    targets = jnp.concatenate([jnp.full((SLOTS,), owner), jnp.full((SLOTS,), partner)])
    offsets = jnp.concatenate([jnp.full((SLOTS,), col), jnp.full((SLOTS,), 1 - col)]) * shard_rows
    slot_ids = jnp.concatenate([jnp.arange(SLOTS), jnp.arange(SLOTS)])
    hit = (block_of[None, :] == targets[:, None]) & (rank[None, :] == slot_ids[:, None])
    valid = jnp.any(hit, axis=1)
    where_row = jnp.sum(jnp.where(hit, local[None, :], 0), axis=1) + offsets
    pick = (where_row[:, None] == jnp.arange(slab.shape[0], dtype=jnp.int32)[None, :]) & valid[:, None]
    rows = jnp.dot(pick.astype(slab.dtype), slab, preferred_element_type=jnp.float32).astype(slab.dtype)
    parts = jnp.dot(rows, gauss, preferred_element_type=jnp.float32)
    own_slots = parts[:SLOTS] + lax.ppermute(parts[SLOTS:], "col", swap)
    slots = lax.all_gather(own_slots, ("row", "col"), tiled=True)

    mine = lax.dynamic_slice_in_dim(slab, col * shard_rows, shard_rows, 0)
    theirs = lax.dynamic_slice_in_dim(slab, (1 - col) * shard_rows, shard_rows, 0)
    other_slab = lax.ppermute(theirs, "col", swap)
    other_gauss = lax.ppermute(gauss, "col", swap)
    sketch = jnp.dot(mine, gauss, preferred_element_type=jnp.float32) + jnp.dot(
        other_slab, other_gauss, preferred_element_type=jnp.float32
    )

    pivot_block = jnp.take(slots, block_of * SLOTS + rank, axis=0)
    share = width // devices
    own_pivots = lax.dynamic_slice_in_dim(pivot_block, owner * share, share, 0)
    factor_rows = solve(sketch, pivot_block, block_inverses)
    return (factor_rows, own_pivots)


def solution(mesh):
    return jax.shard_map(
        on_device,
        mesh=mesh,
        in_specs=(P("row", "col"), P("col", None), P(), P()),
        out_specs=(P(("row", "col"), None), P(("row", "col"), None)),
        check_vma=False,
    )
```

profile of v0, /device:TPU:1, one launch (start us, length us, event | category | flops | bytes accessed | tf_op | source)
XLA Modules:
  0.0 154.5 jit_solution(7297220819678385010)
XLA Ops:
  7.2 0.0 all-gather.2.cloned.1.call-start
  7.2 0.7 add_select_fusion
  7.9 0.5 convert_reduce_fusion
  8.4 0.7 broadcast_clamp_fusion
  9.2 0.1 pad_add_fusion
  9.2 0.2 fusion.11
  9.5 0.2 select_reduce_fusion
  9.7 6.0 %fusion.3 = f32[64,1024]{1,0:T(8,128)S(1)} fusion(bf16[1024,1024]{1,0:T(8,128)(2,1)} %param.5, bf16[4096,1024]{1,0:T(8,128)(2,1)} %param.4, s32[64]{0:T(128)S(1)} %multiply_add_fusion, pred[64]{0:T(512)(128)(4,1)S(1)} %fusion.11), kind=kOutput, calls=%fused_computation.9 | convolution fusion | flops 671678464 | bytes 10748224 | tf_op jit(solution)/shard_map/dot_general | solution.py:88
  15.7 1.5 collective-permute-start.2
  17.2 1.0 collective-permute-done.2
  18.2 0.7 slice_add_fusion
  18.8 0.0 all-gather.2.cloned.1.call-update
  18.9 0.0 copy-start.1
  18.9 0.0 copy-start.2
  18.9 4.8 %constant_dynamic-slice_fusion.1 = bf16[2048,1024]{1,0:T(8,128)(2,1)} fusion(bf16[4096,1024]{1,0:T(8,128)(2,1)} %param.4, s32[]{:T(128)S(6)} %select_n.27), kind=kLoop, calls=%fused_computation.30 | loop fusion | bytes 8388612 | tf_op jit(solution)/shard_map/dynamic_slice | solution.py:93
  23.7 0.4 collective-permute-start
  24.0 0.0 copy-done.1
  24.1 0.1 collective-permute-start.1
  24.2 0.0 copy-done.2
  24.2 6.3 %fusion = f32[2048,1024]{1,0:T(8,128)S(1)} fusion(bf16[1024,1024]{1,0:T(8,128)(2,1)S(1)} %copy-done.1, bf16[4096,1024]{1,0:T(8,128)(2,1)} %param.4, s32[]{:T(128)S(6)} %select_n.26), kind=kOutput, calls=%fused_computation.3 | convolution fusion | flops 4294967296 | bytes 14680068 | tf_op jit(solution)/shard_map/dot_general | solution.py:96
  30.5 3.5 %collective-permute-done.1 = bf16[1024,1024]{1,0:T(8,128)(2,1)} collective-permute-done((bf16[1024,1024]{1,0:T(8,128)(2,1)S(1)}, bf16[1024,1024]{1,0:T(8,128)(2,1)}, u32[]{:S(2)}, u32[]{:S(2)}) %collective-permute-start.1) | collective-permute-done | bytes 2097184 | tf_op jit(solution)/shard_map/ppermute | solution.py:95
  34.0 0.2 collective-permute-done
  34.2 10.9 %convolution_add_fusion.s_ref = f32[2048,1024]{1,0:T(8,128)} fusion(f32[2048,1024]{1,0:T(8,128)S(1)} %fusion, bf16[2048,1024]{1,0:T(8,128)(2,1)} %collective-permute-done, bf16[1024,1024]{1,0:T(8,128)(2,1)} %collective-permute-done.1), kind=kOutput, calls=%fused_computation.6 | convolution fusion | flops 4297064448 | bytes 23068672 | tf_op jit(solution)/shard_map/dot_general | solution.py:96
  45.1 56.8 %all-gather.2.cloned.1.call-done = f32[4096,1024]{1,0:T(8,128)} async-done(((f32[32,1024]{1,0:T(8,128)}), f32[4096,1024]{1,0:T(8,128)}) %all-gather.2.cloned.1.call-update) | async-done | bytes 16777232 | tf_op jit(solution)/shard_map/all_gather | solution.py:90
  101.9 12.1 %gather_fusion = f32[1024,1024]{1,0:T(8,128)} fusion(f32[4096,1024]{1,0:T(8,128)} %all-gather.2.cloned.1.call-done, s32[1024]{0:T(1024)S(1)} %get-tuple-element.2), kind=kCustom, calls=%fused_computation | custom fusion | bytes 8392704 | tf_op jit(solution)/shard_map/jit(_take)/gather | solution.py:100
  114.0 0.0 copy-start
  114.0 2.6 %broadcast_select_fusion.p_ref = f32[1024,1024]{1,0:T(8,128)S(1)} fusion(f32[1024,1024]{1,0:T(8,128)} %gather_fusion, pred[1024]{0:T(1024)(128)(4,1)S(1)} %compare_and_fusion.1), kind=kLoop, calls=%fused_computation.7 | loop fusion | flops 1048576 | bytes 8389632 | tf_op jit(solution)/shard_map/jit(_take)/select_n | solution.py:100
  116.6 0.6 constant_dynamic-slice_fusion
  117.3 0.0 copy-done
  117.3 30.4 %shard_map.59 = f32[2048,1024]{1,0:T(8,128)} custom-call(f32[2048,1024]{1,0:T(8,128)} %convolution_add_fusion.s_ref, f32[1024,1024]{1,0:T(8,128)S(1)} %broadcast_select_fusion.p_ref, f32[8,128,128]{2,1,0:T(8,128)S(1)} %copy-done), custom_call_target="tpu_custom_call" | custom-call | tf_op jit(solution)/shard_map/pallas_call | solution.py:54
  (7 shorter events, 0.0 us)
Async XLA Ops:
  7.2 94.8 %all-gather.2.cloned.1.call-start = ((), (), s32[]{:S(2)}) async-start(), calls=%async_computation | async-start | bytes 16908288 | tf_op jit(solution)/shard_map/all_gather | solution.py:90
  15.7 2.5 %collective-permute-start.2 = (f32[32,1024]{1,0:T(8,128)S(1)}, f32[32,1024]{1,0:T(8,128)S(1)}, u32[]{:S(2)}, u32[]{:S(2)}) collective-permute-start(f32[32,1024]{1,0:T(8,128)S(1)} %slice.11), channel_id=1, source_target_pairs={{0,1},{1,0},{2,3},{3,2},{4,5},{5,4},{6,7},{7,6},{8,9},{9,8},{10,11... | collective-permute-start | bytes 393224 | tf_op jit(solution)/shard_map/ppermute | solution.py:89
  18.9 5.2 %copy-start.1 = (bf16[1024,1024]{1,0:T(8,128)(2,1)S(1)}, bf16[1024,1024]{1,0:T(8,128)(2,1)}, u32[]{:S(2)}) copy-start(bf16[1024,1024]{1,0:T(8,128)(2,1)} %param.5) | copy-start | bytes 6291460
  18.9 5.3 %copy-start.2 = (s32[1024]{0:T(1024)S(1)}, s32[1024]{0:T(1024)}, u32[]{:S(2)}) copy-start(s32[1024]{0:T(1024)} %param.6) | copy-start | bytes 12292
  23.7 10.5 %collective-permute-start = (bf16[2048,1024]{1,0:T(8,128)(2,1)}, bf16[2048,1024]{1,0:T(8,128)(2,1)}, u32[]{:S(2)}, u32[]{:S(2)}) collective-permute-start(bf16[2048,1024]{1,0:T(8,128)(2,1)} %constant_dynamic-slice_fusion.1), channel_id=1, source_target_pairs={{0,1},{1,0},{2,3},{3,2},{4,5},{5,4},{6,7},{7,6},{8,9},{9,8},{10,11... | collective-permute-start | bytes 12582920 | tf_op jit(solution)/shard_map/ppermute | solution.py:94
  24.1 9.9 %collective-permute-start.1 = (bf16[1024,1024]{1,0:T(8,128)(2,1)S(1)}, bf16[1024,1024]{1,0:T(8,128)(2,1)}, u32[]{:S(2)}, u32[]{:S(2)}) collective-permute-start(bf16[1024,1024]{1,0:T(8,128)(2,1)S(1)} %copy-done.1), channel_id=1, source_target_pairs={{0,1},{1,0},{2,3},{3,2},{4,5},{5,4},{6,7},{7,6},{8,9},{9,8},{10,11... | collective-permute-start | bytes 6291464 | tf_op jit(solution)/shard_map/ppermute | solution.py:95
  114.0 3.2 %copy-start = (f32[8,128,128]{2,1,0:T(8,128)S(1)}, f32[8,128,128]{2,1,0:T(8,128)}, u32[]{:S(2)}) copy-start(f32[8,128,128]{2,1,0:T(8,128)} %b_ref.1) | copy-start | bytes 1572868
Sparse Core Ops, SparseCore 0:
  19.0 82.8 all-gather.1
where the time goes:
time: 155 us
  waiting for transfers between devices  61.5 us (40%)
  Pallas kernels  30.4 us (20%)
  matrix products  23.2 us (15%)
  local copies, waits for them, and re-layouts  17.6 us (11%)
  between operations  14.1 us (9%)
  other arithmetic  5.72 us (4%)
  starting transfers between devices  2.05 us (1%)
    all_gather x1, waiting for transfers between devices, on_device(): slots = lax.all_gather(own_slots, ('row', 'col'), tiled=True)  56.8 us
    pallas_call x1, Pallas kernels, solve(): pl.pallas_call(functools.partial(solve_kernel, 1.0 / k ** 0.5), out_shape...  30.4 us
    gather x1, local copies, waits for them, and re-layouts, on_device(): pivot_block = jnp.take(slots, block_of * SLOTS + rank, axis=0)  12.1 us
    dot_general x1, matrix products, on_device(): jnp.dot(other_slab, other_gauss, preferred_element_type=jnp.float32)  10.9 us
    dot_general x1, matrix products, on_device(): jnp.dot(mine, gauss, preferred_element_type=jnp.float32)  6.28 us
    dot_general x1, matrix products, on_device(): parts = jnp.dot(rows, gauss, preferred_element_type=jnp.float32)  5.97 us
    dynamic_slice x1, local copies, waits for them, and re-layouts, on_device(): lax.dynamic_slice_in_dim(slab, (1 - col) * shard_rows, shard_rows, 0)  4.79 us
    ppermute x1, waiting for transfers between devices, on_device(): other_gauss = lax.ppermute(gauss, 'col', swap)  3.47 us
  transfers between devices with their start and end apart: 4, of which 4 were waited for; matrix products, arithmetic and copies ran while one was open for 14% of the time, Pallas kernels for 0%

commit v1 on v0

--- a/solution.py
+++ b/solution.py
@@ -17,14 +17,21 @@
     hi = x.astype(jnp.bfloat16)
     return hi, (x - hi.astype(jnp.float32)).astype(jnp.bfloat16)
 
-
-def solve_kernel(factor, s_ref, p_ref, b_ref, f_ref, pcat, bcat, g):
+def solve_kernel(factor, share, idx_ref, own_ref, s_ref, slots_hbm, b_ref, f_ref, piv_ref, pbuf, pcat, bcat, g, sem):
     nb = s_ref.shape[1] // BLK
+    k = pbuf.shape[0]
 
     @pl.when(pl.program_id(0) == 0)
     def _():
+        def fetch(r, carry):
+            pltpu.make_async_copy(slots_hbm.at[pl.ds(idx_ref[r], 1)], pbuf.at[pl.ds(r, 1)], sem).start()
+            return carry
+
+        lax.fori_loop(0, k, fetch, 0, unroll=8)
+        pltpu.make_async_copy(slots_hbm.at[pl.ds(0, k)], pbuf, sem).wait()
+        piv_ref[...] = pbuf[pl.ds(pl.multiple_of(own_ref[0] * share, share), share), :]
         for i in range(nb):
-            hi, lo = split(p_ref[i * BLK:(i + 1) * BLK, :] * factor)
+            hi, lo = split(pbuf[i * BLK:(i + 1) * BLK, :] * factor)
             pcat[3 * i * BLK:(3 * i + 1) * BLK, :] = hi
             pcat[(3 * i + 1) * BLK:(3 * i + 2) * BLK, :] = lo
             pcat[(3 * i + 2) * BLK:(3 * i + 3) * BLK, :] = hi
@@ -32,6 +39,7 @@
             bcat[i, 0:BLK, :] = bh
             bcat[i, BLK:2 * BLK, :] = bl
             bcat[i, 2 * BLK:3 * BLK, :] = bh
+
     for j in range(nb):
         cols = slice(j * BLK, (j + 1) * BLK)
         acc = s_ref[:, cols]
@@ -47,19 +55,28 @@
             g[:, (3 * j + 2) * BLK:(3 * j + 3) * BLK] = o_lo
 
 
-def solve(sketch, pivot_block, block_inverses):
+def solve(sketch, slots, idx, owner, share, block_inverses):
     rows, k = sketch.shape
     nb = k // BLK
-    full = lambda shape: pl.BlockSpec(shape, lambda i: (0,) * len(shape))
+    full = lambda shape: pl.BlockSpec(shape, lambda i, *_: (0,) * len(shape))
     return pl.pallas_call(
-        functools.partial(solve_kernel, 1.0 / k**0.5),
-        out_shape=jax.ShapeDtypeStruct((rows, k), jnp.float32),
-        grid=(rows // TM,),
-        in_specs=[pl.BlockSpec((TM, k), lambda i: (i, 0)), full((k, k)), full(block_inverses.shape)],
-        out_specs=pl.BlockSpec((TM, k), lambda i: (i, 0)),
-        scratch_shapes=[pltpu.VMEM((3 * k, k), jnp.bfloat16), pltpu.VMEM((nb, 3 * BLK, BLK), jnp.bfloat16), pltpu.VMEM((TM, 3 * k), jnp.bfloat16)],
-        compiler_params=pltpu.CompilerParams(vmem_limit_bytes=48 * 1024 * 1024),
-    )(sketch, pivot_block, block_inverses)
+        functools.partial(solve_kernel, 1.0 / k**0.5, share),
+        out_shape=(jax.ShapeDtypeStruct((rows, k), jnp.float32), jax.ShapeDtypeStruct((share, k), jnp.float32)),
+        grid_spec=pltpu.PrefetchScalarGridSpec(
+            num_scalar_prefetch=2,
+            grid=(rows // TM,),
+            in_specs=[pl.BlockSpec((TM, k), lambda i, *_: (i, 0)), pl.BlockSpec(memory_space=pl.ANY), full(block_inverses.shape)],
+            out_specs=[pl.BlockSpec((TM, k), lambda i, *_: (i, 0)), full((share, k))],
+            scratch_shapes=[
+                pltpu.VMEM((k, k), jnp.float32),
+                pltpu.VMEM((3 * k, k), jnp.bfloat16),
+                pltpu.VMEM((nb, 3 * BLK, BLK), jnp.bfloat16),
+                pltpu.VMEM((TM, 3 * k), jnp.bfloat16),
+                pltpu.SemaphoreType.DMA,
+            ],
+        ),
+        compiler_params=pltpu.CompilerParams(vmem_limit_bytes=56 * 1024 * 1024),
+    )(idx, owner, sketch, slots, block_inverses)
 
 
 def on_device(slab, gauss, pivots, block_inverses):
@@ -97,10 +114,8 @@
         other_slab, other_gauss, preferred_element_type=jnp.float32
     )
 
-    pivot_block = jnp.take(slots, block_of * SLOTS + rank, axis=0)
     share = width // devices
-    own_pivots = lax.dynamic_slice_in_dim(pivot_block, owner * share, share, 0)
-    factor_rows = solve(sketch, pivot_block, block_inverses)
+    factor_rows, own_pivots = solve(sketch, slots, block_of * SLOTS + rank, owner[None], share, block_inverses)
     return (factor_rows, own_pivots)
 
 

time: 155 us -> 147 us (0.948)
  local copies, waits for them, and re-layouts: 17.6 us -> 4.82 us
  Pallas kernels: 30.4 us -> 37.8 us
  other arithmetic: 5.72 us -> 3.69 us
    gather x1 -> x0, local copies, waits for them, and re-layouts: 12.1 us -> none  [on_device(): pivot_block = jnp.take(slots, block_of * SLOTS + rank, axis=0)]
    pallas_call x1, Pallas kernels: 30.4 us -> 37.8 us  [solve(): pl.pallas_call(functools.partial(solve_kernel, 1.0 / k ** 0.5, share), ou...]
    select_n x1 -> x0, other arithmetic: 2.6 us -> none  [on_device(): pivot_block = jnp.take(slots, block_of * SLOTS + rank, axis=0)]
  transfers between devices with their start and end apart: 4 -> 4, of which waited for: 4 -> 4; matrix products, arithmetic and copies ran while one was open for 14% -> 15% of each run, Pallas kernels for 0% -> 0%
where the time goes in v1:
time: 147 us
  waiting for transfers between devices  61.5 us (42%)
  Pallas kernels  37.8 us (26%)
  matrix products  23.2 us (16%)
  between operations  14.1 us (10%)
  local copies, waits for them, and re-layouts  4.82 us (3%)
  other arithmetic  3.69 us (3%)
  starting transfers between devices  2.05 us (1%)
    all_gather x1, waiting for transfers between devices, on_device(): slots = lax.all_gather(own_slots, ('row', 'col'), tiled=True)  56.8 us
    pallas_call x1, Pallas kernels, solve(): pl.pallas_call(functools.partial(solve_kernel, 1.0 / k ** 0.5, share), ou...  37.8 us
    dot_general x1, matrix products, on_device(): jnp.dot(other_slab, other_gauss, preferred_element_type=jnp.float32)  10.9 us
    dot_general x1, matrix products, on_device(): jnp.dot(mine, gauss, preferred_element_type=jnp.float32)  6.28 us
    dot_general x1, matrix products, on_device(): parts = jnp.dot(rows, gauss, preferred_element_type=jnp.float32)  5.97 us
    dynamic_slice x1, local copies, waits for them, and re-layouts, on_device(): lax.dynamic_slice_in_dim(slab, (1 - col) * shard_rows, shard_rows, 0)  4.79 us
    ppermute x1, waiting for transfers between devices, on_device(): other_gauss = lax.ppermute(gauss, 'col', swap)  3.49 us
  transfers between devices with their start and end apart: 4, of which 4 were waited for; matrix products, arithmetic and copies ran while one was open for 15% of the time, Pallas kernels for 0%

profile of v1, /device:TPU:1, one launch (start us, length us, event | category | flops | bytes accessed | tf_op | source)
XLA Modules:
  0.0 147.1 jit_solution(3998878397674159444)
XLA Ops:
  7.2 0.0 all-gather.2.cloned.1.call-start
  7.2 0.1 pad_add_fusion
  7.3 0.7 add_select_fusion
  8.0 0.5 convert_reduce_fusion
  8.5 1.3 multiply_subtract_fusion
  9.8 0.2 fusion.11
  10.1 0.2 select_reduce_fusion
  10.3 6.0 %fusion.3 = f32[64,1024]{1,0:T(8,128)S(1)} fusion(bf16[1024,1024]{1,0:T(8,128)(2,1)} %param.5, bf16[4096,1024]{1,0:T(8,128)(2,1)} %param.4, s32[64]{0:T(128)S(1)} %multiply_add_fusion.1, pred[64]{0:T(512)(128)(4,1)S(1)} %fusion.11), kind=kOutput, calls=%fused_computation.7 | convolution fusion | flops 671678464 | bytes 10748224 | tf_op jit(solution)/shard_map/dot_general | solution.py:105
  16.3 1.5 %collective-permute-start.2 = (f32[32,1024]{1,0:T(8,128)S(1)}, f32[32,1024]{1,0:T(8,128)S(1)}, u32[]{:S(2)}, u32[]{:S(2)}) collective-permute-start(f32[32,1024]{1,0:T(8,128)S(1)} %slice.9), channel_id=1, source_target_pairs={{0,1},{1,0},{2,3},{3,2},{4,5},{5,4},{6,7},{7,6},{8,9},{9,8},{10,11... | collective-permute-start | bytes 393224 | tf_op jit(solution)/shard_map/ppermute | solution.py:106
  17.8 1.0 collective-permute-done.2
  18.8 0.7 slice_add_fusion
  19.4 0.0 all-gather.2.cloned.1.call-update
  19.5 0.0 copy-start
  19.5 4.8 %constant_dynamic-slice_fusion = bf16[2048,1024]{1,0:T(8,128)(2,1)} fusion(bf16[4096,1024]{1,0:T(8,128)(2,1)} %param.4, s32[]{:T(128)S(6)} %select_n.17), kind=kLoop, calls=%fused_computation.27 | loop fusion | bytes 8388612 | tf_op jit(solution)/shard_map/dynamic_slice | solution.py:110
  24.3 0.4 collective-permute-start
  24.6 0.0 copy-done
  24.6 0.1 collective-permute-start.1
  24.8 6.3 %fusion = f32[2048,1024]{1,0:T(8,128)S(1)} fusion(bf16[1024,1024]{1,0:T(8,128)(2,1)S(1)} %copy-done, bf16[4096,1024]{1,0:T(8,128)(2,1)} %param.4, s32[]{:T(128)S(6)} %select_n.16), kind=kOutput, calls=%fused_computation | convolution fusion | flops 4294967296 | bytes 14680068 | tf_op jit(solution)/shard_map/dot_general | solution.py:113
  31.1 3.5 %collective-permute-done.1 = bf16[1024,1024]{1,0:T(8,128)(2,1)} collective-permute-done((bf16[1024,1024]{1,0:T(8,128)(2,1)S(1)}, bf16[1024,1024]{1,0:T(8,128)(2,1)}, u32[]{:S(2)}, u32[]{:S(2)}) %collective-permute-start.1) | collective-permute-done | bytes 2097184 | tf_op jit(solution)/shard_map/ppermute | solution.py:112
  34.5 0.2 collective-permute-done
  34.7 10.9 %convolution_add_fusion.s_ref = f32[2048,1024]{1,0:T(8,128)} fusion(f32[2048,1024]{1,0:T(8,128)S(1)} %fusion, bf16[2048,1024]{1,0:T(8,128)(2,1)} %collective-permute-done, bf16[1024,1024]{1,0:T(8,128)(2,1)} %collective-permute-done.1), kind=kOutput, calls=%fused_computation.5 | convolution fusion | flops 4297064448 | bytes 23068672 | tf_op jit(solution)/shard_map/dot_general | solution.py:113
  45.7 56.8 %all-gather.2.cloned.1.call-done.slots_hbm = f32[4096,1024]{1,0:T(8,128)} async-done(((f32[32,1024]{1,0:T(8,128)}), f32[4096,1024]{1,0:T(8,128)}) %all-gather.2.cloned.1.call-update) | async-done | bytes 16777232 | tf_op jit(solution)/shard_map/all_gather | solution.py:107
  102.5 37.8 %shard_map.59 = (f32[2048,1024]{1,0:T(8,128)}, f32[8,1024]{1,0:T(8,128)}) custom-call(s32[1024]{0:T(1024)} %get-tuple-element.3.idx_ref, s32[1]{0:T(128)} %bitcast.own_ref, f32[2048,1024]{1,0:T(8,128)} %convolution_add_fusion.s_ref, f32[4096,1024]{1,0:T(8,128)} %all-gather.2.cloned.1.call-done.slots_hbm, f32[8,128,128]{2,1,0:T(8,128)} %b_ref.1), custom_call_target="tpu_custom_call" | custom-call | tf_op jit(solution)/shard_map/pallas_call | solution.py:62
  (6 shorter events, 0.0 us)
Async XLA Ops:
  7.2 95.3 %all-gather.2.cloned.1.call-start = ((), (), s32[]{:S(2)}) async-start(), calls=%async_computation | async-start | bytes 16908288 | tf_op jit(solution)/shard_map/all_gather | solution.py:107
  16.3 2.5 %collective-permute-start.2 = (f32[32,1024]{1,0:T(8,128)S(1)}, f32[32,1024]{1,0:T(8,128)S(1)}, u32[]{:S(2)}, u32[]{:S(2)}) collective-permute-start(f32[32,1024]{1,0:T(8,128)S(1)} %slice.9), channel_id=1, source_target_pairs={{0,1},{1,0},{2,3},{3,2},{4,5},{5,4},{6,7},{7,6},{8,9},{9,8},{10,11... | collective-permute-start | bytes 393224 | tf_op jit(solution)/shard_map/ppermute | solution.py:106
  19.5 5.2 %copy-start = (bf16[1024,1024]{1,0:T(8,128)(2,1)S(1)}, bf16[1024,1024]{1,0:T(8,128)(2,1)}, u32[]{:S(2)}) copy-start(bf16[1024,1024]{1,0:T(8,128)(2,1)} %param.5) | copy-start | bytes 6291460
  24.3 10.5 %collective-permute-start = (bf16[2048,1024]{1,0:T(8,128)(2,1)}, bf16[2048,1024]{1,0:T(8,128)(2,1)}, u32[]{:S(2)}, u32[]{:S(2)}) collective-permute-start(bf16[2048,1024]{1,0:T(8,128)(2,1)} %constant_dynamic-slice_fusion), channel_id=1, source_target_pairs={{0,1},{1,0},{2,3},{3,2},{4,5},{5,4},{6,7},{7,6},{8,9},{9,8},{10,11... | collective-permute-start | bytes 12582920 | tf_op jit(solution)/shard_map/ppermute | solution.py:111
  24.6 9.9 %collective-permute-start.1 = (bf16[1024,1024]{1,0:T(8,128)(2,1)S(1)}, bf16[1024,1024]{1,0:T(8,128)(2,1)}, u32[]{:S(2)}, u32[]{:S(2)}) collective-permute-start(bf16[1024,1024]{1,0:T(8,128)(2,1)S(1)} %copy-done), channel_id=1, source_target_pairs={{0,1},{1,0},{2,3},{3,2},{4,5},{5,4},{6,7},{7,6},{8,9},{9,8},{10,11... | collective-permute-start | bytes 6291464 | tf_op jit(solution)/shard_map/ppermute | solution.py:112
Sparse Core Ops, SparseCore 0:
  19.6 82.8 all-gather.1

commit v2 on v1

--- a/solution.py
+++ b/solution.py
@@ -17,9 +17,17 @@
     hi = x.astype(jnp.bfloat16)
     return hi, (x - hi.astype(jnp.float32)).astype(jnp.bfloat16)
 
-def solve_kernel(factor, share, idx_ref, own_ref, s_ref, slots_hbm, b_ref, f_ref, piv_ref, pbuf, pcat, bcat, g, sem):
+def dot3(a, b):
+    a_hi, a_lo = split(a)
+    b_hi, b_lo = split(b)
+    d = functools.partial(jnp.dot, preferred_element_type=jnp.float32)
+    return d(a_hi, b_hi) + (d(a_hi, b_lo) + d(a_lo, b_hi))
+
+
+def solve_kernel(factor, share, idx_ref, own_ref, s_ref, slots_hbm, b_ref, f_ref, piv_ref, pbuf, pcat, tcat, g, sem):
     nb = s_ref.shape[1] // BLK
     k = pbuf.shape[0]
+    pw = 2 * BLK
 
     @pl.when(pl.program_id(0) == 0)
     def _():
@@ -35,24 +43,34 @@
             pcat[3 * i * BLK:(3 * i + 1) * BLK, :] = hi
             pcat[(3 * i + 1) * BLK:(3 * i + 2) * BLK, :] = lo
             pcat[(3 * i + 2) * BLK:(3 * i + 3) * BLK, :] = hi
-            bh, bl = split(b_ref[i])
-            bcat[i, 0:BLK, :] = bh
-            bcat[i, BLK:2 * BLK, :] = bl
-            bcat[i, 2 * BLK:3 * BLK, :] = bh
+        for q in range(nb // 2):
+            a, b = 2 * q, 2 * q + 1
+            cross = -dot3(dot3(b_ref[a], pbuf[a * BLK:b * BLK, b * BLK:(b + 1) * BLK] * factor), b_ref[b])
+            zero = jnp.zeros((BLK, BLK), jnp.float32)
+            panel = jnp.concatenate(
+                [jnp.concatenate([b_ref[a], cross], axis=1), jnp.concatenate([zero, b_ref[b]], axis=1)], axis=0
+            )
+            hi, lo = split(panel)
+            tcat[q, 0:pw, :] = hi
+            tcat[q, pw:2 * pw, :] = lo
+            tcat[q, 2 * pw:3 * pw, :] = hi
 
-    for j in range(nb):
-        cols = slice(j * BLK, (j + 1) * BLK)
+    for q in range(nb // 2):
+        cols = slice(q * pw, (q + 1) * pw)
         acc = s_ref[:, cols]
-        if j > 0:
-            acc = acc - jnp.dot(g[:, : 3 * j * BLK], pcat[: 3 * j * BLK, cols], preferred_element_type=jnp.float32)
+        if q > 0:
+            acc = acc - jnp.dot(g[:, : 3 * q * pw], pcat[: 3 * q * pw, cols], preferred_element_type=jnp.float32)
         a_hi, a_lo = split(acc)
-        out = jnp.dot(jnp.concatenate([a_hi, a_hi, a_lo], axis=1), bcat[j], preferred_element_type=jnp.float32)
+        out = jnp.dot(jnp.concatenate([a_hi, a_hi, a_lo], axis=1), tcat[q], preferred_element_type=jnp.float32)
         f_ref[:, cols] = out
-        if j + 1 < nb:
+        if q + 1 < nb // 2:
             o_hi, o_lo = split(out)
-            g[:, 3 * j * BLK:(3 * j + 1) * BLK] = o_hi
-            g[:, (3 * j + 1) * BLK:(3 * j + 2) * BLK] = o_hi
-            g[:, (3 * j + 2) * BLK:(3 * j + 3) * BLK] = o_lo
+            for h in range(2):
+                blk = 2 * q + h
+                part = slice(h * BLK, (h + 1) * BLK)
+                g[:, 3 * blk * BLK:(3 * blk + 1) * BLK] = o_hi[:, part]
+                g[:, (3 * blk + 1) * BLK:(3 * blk + 2) * BLK] = o_hi[:, part]
+                g[:, (3 * blk + 2) * BLK:(3 * blk + 3) * BLK] = o_lo[:, part]
 
 
 def solve(sketch, slots, idx, owner, share, block_inverses):
@@ -70,7 +88,7 @@
             scratch_shapes=[
                 pltpu.VMEM((k, k), jnp.float32),
                 pltpu.VMEM((3 * k, k), jnp.bfloat16),
-                pltpu.VMEM((nb, 3 * BLK, BLK), jnp.bfloat16),
+                pltpu.VMEM((nb // 2, 6 * BLK, 2 * BLK), jnp.bfloat16),
                 pltpu.VMEM((TM, 3 * k), jnp.bfloat16),
                 pltpu.SemaphoreType.DMA,
             ],

time: 147 us -> 136 us (0.925)
  Pallas kernels: 37.8 us -> 26.8 us
    pallas_call x1, Pallas kernels: 37.8 us -> 26.8 us  [solve(): pl.pallas_call(functools.partial(solve_kernel, 1.0 / k ** 0.5, share), ou...]
  transfers between devices with their start and end apart: 4 -> 4, of which waited for: 4 -> 4; matrix products, arithmetic and copies ran while one was open for 15% -> 16% of each run, Pallas kernels for 0% -> 0%
where the time goes in v2:
time: 136 us
  waiting for transfers between devices  61.5 us (45%)
  Pallas kernels  26.8 us (20%)
  matrix products  23.2 us (17%)
  between operations  14.1 us (10%)
  local copies, waits for them, and re-layouts  4.82 us (4%)
  other arithmetic  3.69 us (3%)
  starting transfers between devices  2.05 us (2%)
    all_gather x1, waiting for transfers between devices, on_device(): slots = lax.all_gather(own_slots, ('row', 'col'), tiled=True)  56.8 us
    pallas_call x1, Pallas kernels, solve(): pl.pallas_call(functools.partial(solve_kernel, 1.0 / k ** 0.5, share), ou...  26.8 us
    dot_general x1, matrix products, on_device(): jnp.dot(other_slab, other_gauss, preferred_element_type=jnp.float32)  10.9 us
    dot_general x1, matrix products, on_device(): jnp.dot(mine, gauss, preferred_element_type=jnp.float32)  6.27 us
    dot_general x1, matrix products, on_device(): parts = jnp.dot(rows, gauss, preferred_element_type=jnp.float32)  5.97 us
    dynamic_slice x1, local copies, waits for them, and re-layouts, on_device(): lax.dynamic_slice_in_dim(slab, (1 - col) * shard_rows, shard_rows, 0)  4.79 us
    ppermute x1, waiting for transfers between devices, on_device(): other_gauss = lax.ppermute(gauss, 'col', swap)  3.49 us
  transfers between devices with their start and end apart: 4, of which 4 were waited for; matrix products, arithmetic and copies ran while one was open for 16% of the time, Pallas kernels for 0%

profile of v2, /device:TPU:1, one launch (start us, length us, event | category | flops | bytes accessed | tf_op | source)
XLA Modules:
  0.0 136.1 jit_solution(16401144352436870802)
XLA Ops:
  7.2 0.0 all-gather.2.cloned.1.call-start
  7.2 0.1 pad_add_fusion
  7.3 0.7 add_select_fusion
  8.0 0.5 convert_reduce_fusion
  8.5 1.3 multiply_subtract_fusion
  9.8 0.2 fusion.11
  10.1 0.2 select_reduce_fusion
  10.3 6.0 %fusion.3 = f32[64,1024]{1,0:T(8,128)S(1)} fusion(bf16[1024,1024]{1,0:T(8,128)(2,1)} %param.5, bf16[4096,1024]{1,0:T(8,128)(2,1)} %param.4, s32[64]{0:T(128)S(1)} %multiply_add_fusion.1, pred[64]{0:T(512)(128)(4,1)S(1)} %fusion.11), kind=kOutput, calls=%fused_computation.7 | convolution fusion | flops 671678464 | bytes 10748224 | tf_op jit(solution)/shard_map/dot_general | solution.py:123
  16.3 1.5 %collective-permute-start.2 = (f32[32,1024]{1,0:T(8,128)S(1)}, f32[32,1024]{1,0:T(8,128)S(1)}, u32[]{:S(2)}, u32[]{:S(2)}) collective-permute-start(f32[32,1024]{1,0:T(8,128)S(1)} %slice.9), channel_id=1, source_target_pairs={{0,1},{1,0},{2,3},{3,2},{4,5},{5,4},{6,7},{7,6},{8,9},{9,8},{10,11... | collective-permute-start | bytes 393224 | tf_op jit(solution)/shard_map/ppermute | solution.py:124
  17.8 1.0 collective-permute-done.2
  18.8 0.7 slice_add_fusion
  19.4 0.0 all-gather.2.cloned.1.call-update
  19.5 0.0 copy-start
  19.5 4.8 %constant_dynamic-slice_fusion = bf16[2048,1024]{1,0:T(8,128)(2,1)} fusion(bf16[4096,1024]{1,0:T(8,128)(2,1)} %param.4, s32[]{:T(128)S(6)} %select_n.17), kind=kLoop, calls=%fused_computation.27 | loop fusion | bytes 8388612 | tf_op jit(solution)/shard_map/dynamic_slice | solution.py:128
  24.3 0.4 collective-permute-start
  24.6 0.0 copy-done
  24.6 0.1 collective-permute-start.1
  24.8 6.3 %fusion = f32[2048,1024]{1,0:T(8,128)S(1)} fusion(bf16[1024,1024]{1,0:T(8,128)(2,1)S(1)} %copy-done, bf16[4096,1024]{1,0:T(8,128)(2,1)} %param.4, s32[]{:T(128)S(6)} %select_n.16), kind=kOutput, calls=%fused_computation | convolution fusion | flops 4294967296 | bytes 14680068 | tf_op jit(solution)/shard_map/dot_general | solution.py:131
  31.1 3.5 %collective-permute-done.1 = bf16[1024,1024]{1,0:T(8,128)(2,1)} collective-permute-done((bf16[1024,1024]{1,0:T(8,128)(2,1)S(1)}, bf16[1024,1024]{1,0:T(8,128)(2,1)}, u32[]{:S(2)}, u32[]{:S(2)}) %collective-permute-start.1) | collective-permute-done | bytes 2097184 | tf_op jit(solution)/shard_map/ppermute | solution.py:130
  34.5 0.2 collective-permute-done
  34.7 10.9 %convolution_add_fusion.s_ref = f32[2048,1024]{1,0:T(8,128)} fusion(f32[2048,1024]{1,0:T(8,128)S(1)} %fusion, bf16[2048,1024]{1,0:T(8,128)(2,1)} %collective-permute-done, bf16[1024,1024]{1,0:T(8,128)(2,1)} %collective-permute-done.1), kind=kOutput, calls=%fused_computation.5 | convolution fusion | flops 4297064448 | bytes 23068672 | tf_op jit(solution)/shard_map/dot_general | solution.py:131
  45.7 56.8 %all-gather.2.cloned.1.call-done.slots_hbm = f32[4096,1024]{1,0:T(8,128)} async-done(((f32[32,1024]{1,0:T(8,128)}), f32[4096,1024]{1,0:T(8,128)}) %all-gather.2.cloned.1.call-update) | async-done | bytes 16777232 | tf_op jit(solution)/shard_map/all_gather | solution.py:125
  102.5 26.8 %shard_map.59 = (f32[2048,1024]{1,0:T(8,128)}, f32[8,1024]{1,0:T(8,128)}) custom-call(s32[1024]{0:T(1024)} %get-tuple-element.3.idx_ref, s32[1]{0:T(128)} %bitcast.own_ref, f32[2048,1024]{1,0:T(8,128)} %convolution_add_fusion.s_ref, f32[4096,1024]{1,0:T(8,128)} %all-gather.2.cloned.1.call-done.slots_hbm, f32[8,128,128]{2,1,0:T(8,128)} %b_ref.1), custom_call_target="tpu_custom_call" | custom-call | tf_op jit(solution)/shard_map/pallas_call | solution.py:80
  (6 shorter events, 0.0 us)
Async XLA Ops:
  7.2 95.3 %all-gather.2.cloned.1.call-start = ((), (), s32[]{:S(2)}) async-start(), calls=%async_computation | async-start | bytes 16908288 | tf_op jit(solution)/shard_map/all_gather | solution.py:125
  16.3 2.5 %collective-permute-start.2 = (f32[32,1024]{1,0:T(8,128)S(1)}, f32[32,1024]{1,0:T(8,128)S(1)}, u32[]{:S(2)}, u32[]{:S(2)}) collective-permute-start(f32[32,1024]{1,0:T(8,128)S(1)} %slice.9), channel_id=1, source_target_pairs={{0,1},{1,0},{2,3},{3,2},{4,5},{5,4},{6,7},{7,6},{8,9},{9,8},{10,11... | collective-permute-start | bytes 393224 | tf_op jit(solution)/shard_map/ppermute | solution.py:124
  19.5 5.2 %copy-start = (bf16[1024,1024]{1,0:T(8,128)(2,1)S(1)}, bf16[1024,1024]{1,0:T(8,128)(2,1)}, u32[]{:S(2)}) copy-start(bf16[1024,1024]{1,0:T(8,128)(2,1)} %param.5) | copy-start | bytes 6291460
  24.3 10.5 %collective-permute-start = (bf16[2048,1024]{1,0:T(8,128)(2,1)}, bf16[2048,1024]{1,0:T(8,128)(2,1)}, u32[]{:S(2)}, u32[]{:S(2)}) collective-permute-start(bf16[2048,1024]{1,0:T(8,128)(2,1)} %constant_dynamic-slice_fusion), channel_id=1, source_target_pairs={{0,1},{1,0},{2,3},{3,2},{4,5},{5,4},{6,7},{7,6},{8,9},{9,8},{10,11... | collective-permute-start | bytes 12582920 | tf_op jit(solution)/shard_map/ppermute | solution.py:129
  24.6 9.9 %collective-permute-start.1 = (bf16[1024,1024]{1,0:T(8,128)(2,1)S(1)}, bf16[1024,1024]{1,0:T(8,128)(2,1)}, u32[]{:S(2)}, u32[]{:S(2)}) collective-permute-start(bf16[1024,1024]{1,0:T(8,128)(2,1)S(1)} %copy-done), channel_id=1, source_target_pairs={{0,1},{1,0},{2,3},{3,2},{4,5},{5,4},{6,7},{7,6},{8,9},{9,8},{10,11... | collective-permute-start | bytes 6291464 | tf_op jit(solution)/shard_map/ppermute | solution.py:130
Sparse Core Ops, SparseCore 0:
  19.6 82.8 all-gather.1

commit v3 on v2

--- a/solution.py
+++ b/solution.py
@@ -97,6 +97,50 @@
     )(idx, owner, sketch, slots, block_inverses)
 
 
+def exchange_kernel(slab_hbm, gauss_hbm, slab_out, gauss_out, sems):
+    row = lax.axis_index("row")
+    partner = 1 - lax.axis_index("col")
+    mesh_ids = pl.DeviceIdType.MESH
+    barrier = pltpu.get_barrier_semaphore()
+    pl.semaphore_signal(barrier, 1, device_id=(row, partner), device_id_type=mesh_ids)
+    pl.semaphore_wait(barrier, 1)
+    rows = slab_out.shape[0]
+    copies = [
+        pltpu.make_async_remote_copy(
+            src_ref=slab_hbm.at[pl.ds(pl.multiple_of(partner * rows, rows), rows)],
+            dst_ref=slab_out,
+            send_sem=sems.at[0],
+            recv_sem=sems.at[1],
+            device_id=(row, partner),
+            device_id_type=mesh_ids,
+        ),
+        pltpu.make_async_remote_copy(
+            src_ref=gauss_hbm,
+            dst_ref=gauss_out,
+            send_sem=sems.at[2],
+            recv_sem=sems.at[3],
+            device_id=(row, partner),
+            device_id_type=mesh_ids,
+        ),
+    ]
+    for copy in copies:
+        copy.start()
+    for copy in copies:
+        copy.wait()
+
+
+def exchange(slab, gauss, rows):
+    anywhere = pl.BlockSpec(memory_space=pl.ANY)
+    return pl.pallas_call(
+        exchange_kernel,
+        out_shape=(jax.ShapeDtypeStruct((rows, slab.shape[1]), slab.dtype), jax.ShapeDtypeStruct(gauss.shape, gauss.dtype)),
+        in_specs=[anywhere, anywhere],
+        out_specs=[anywhere, anywhere],
+        scratch_shapes=[pltpu.SemaphoreType.DMA((4,))],
+        compiler_params=pltpu.CompilerParams(collective_id=0, has_side_effects=True),
+    )(slab, gauss)
+
+
 def on_device(slab, gauss, pivots, block_inverses):
     col_count = lax.axis_size("col")
     devices = lax.axis_size("row") * col_count
@@ -116,18 +160,14 @@
     offsets = jnp.concatenate([jnp.full((SLOTS,), col), jnp.full((SLOTS,), 1 - col)]) * shard_rows
     slot_ids = jnp.concatenate([jnp.arange(SLOTS), jnp.arange(SLOTS)])
     hit = (block_of[None, :] == targets[:, None]) & (rank[None, :] == slot_ids[:, None])
-    valid = jnp.any(hit, axis=1)
     where_row = jnp.sum(jnp.where(hit, local[None, :], 0), axis=1) + offsets
-    pick = (where_row[:, None] == jnp.arange(slab.shape[0], dtype=jnp.int32)[None, :]) & valid[:, None]
-    rows = jnp.dot(pick.astype(slab.dtype), slab, preferred_element_type=jnp.float32).astype(slab.dtype)
+    rows = jnp.take(slab, where_row, axis=0, mode="clip")
     parts = jnp.dot(rows, gauss, preferred_element_type=jnp.float32)
     own_slots = parts[:SLOTS] + lax.ppermute(parts[SLOTS:], "col", swap)
     slots = lax.all_gather(own_slots, ("row", "col"), tiled=True)
 
     mine = lax.dynamic_slice_in_dim(slab, col * shard_rows, shard_rows, 0)
-    theirs = lax.dynamic_slice_in_dim(slab, (1 - col) * shard_rows, shard_rows, 0)
-    other_slab = lax.ppermute(theirs, "col", swap)
-    other_gauss = lax.ppermute(gauss, "col", swap)
+    other_slab, other_gauss = exchange(slab, gauss, shard_rows)
     sketch = jnp.dot(mine, gauss, preferred_element_type=jnp.float32) + jnp.dot(
         other_slab, other_gauss, preferred_element_type=jnp.float32
     )

time: 136 us -> 138 us (1.015)
  Pallas kernels: 26.8 us -> 37.3 us
  matrix products: 23.2 us -> 15.2 us
    pallas_call x0 -> x1, Pallas kernels: none -> 10.5 us  [exchange(): pl.pallas_call(exchange_kernel, out_shape=(jax.ShapeDtypeStruct((rows, sl...]
    gather x0 -> x1, local copies, waits for them, and re-layouts: none -> 5.26 us  [on_device(): rows = jnp.take(slab, where_row, axis=0, mode='clip')]
    dynamic_slice x1 -> x0, local copies, waits for them, and re-layouts: 4.79 us -> none  [on_device(): lax.dynamic_slice_in_dim(slab, (1 - col) * shard_rows, shard_rows, 0)]
    dot_general x1, matrix products: 10.9 us -> 6.7 us  [on_device(): jnp.dot(other_slab, other_gauss, preferred_element_type=jnp.float32)]
    dot_general x1, matrix products: 5.97 us -> 2.07 us  [on_device(): parts = jnp.dot(rows, gauss, preferred_element_type=jnp.float32)]
    ppermute x2 -> x0, waiting for transfers between devices: 3.69 us -> none  [the longest x1 3.49 us: on_device(): other_gauss = lax.ppermute(gauss, 'col', swap)]
    all_gather x1, waiting for transfers between devices: 56.8 us -> 59.3 us  [on_device(): slots = lax.all_gather(own_slots, ('row', 'col'), tiled=True)]
  transfers between devices with their start and end apart: 4 -> 2, of which waited for: 4 -> 2; matrix products, arithmetic and copies ran while one was open for 16% -> 10% of each run, Pallas kernels for 0% -> 8%
where the time goes in v3:
time: 138 us; the launch traced here: 137 us
  waiting for transfers between devices  60.3 us (44%)
  Pallas kernels  37.3 us (27%)
  matrix products  15.2 us (11%)
  between operations  14.2 us (10%)
  local copies, waits for them, and re-layouts  5.3 us (4%)
  other arithmetic  3.47 us (3%)
  starting transfers between devices  1.54 us (1%)
    all_gather x1, waiting for transfers between devices, on_device(): slots = lax.all_gather(own_slots, ('row', 'col'), tiled=True)  59.3 us
    pallas_call x1, Pallas kernels, solve(): pl.pallas_call(functools.partial(solve_kernel, 1.0 / k ** 0.5, share), ou...  26.8 us
    pallas_call x1, Pallas kernels, exchange(): pl.pallas_call(exchange_kernel, out_shape=(jax.ShapeDtypeStruct((rows, sl...  10.5 us
    dot_general x1, matrix products, on_device(): jnp.dot(other_slab, other_gauss, preferred_element_type=jnp.float32)  6.7 us
    dot_general x1, matrix products, on_device(): jnp.dot(mine, gauss, preferred_element_type=jnp.float32)  6.43 us
    gather x1, local copies, waits for them, and re-layouts, on_device(): rows = jnp.take(slab, where_row, axis=0, mode='clip')  5.26 us
  transfers between devices with their start and end apart: 2, of which 2 were waited for; matrix products, arithmetic and copies ran while one was open for 10% of the time, Pallas kernels for 8%

profile of v3, /device:TPU:1, one launch (start us, length us, event | category | flops | bytes accessed | tf_op | source)
XLA Modules:
  0.0 137.3 jit_solution(6343276512143954801)
XLA Ops:
  7.2 0.0 all-gather.2.cloned.1.call-start
  7.2 0.1 pad_add_fusion
  7.3 0.7 add_select_fusion
  8.0 0.5 convert_reduce_fusion
  8.5 1.3 multiply_subtract_fusion
  9.8 0.2 select_reduce_fusion
  10.1 5.3 %gather_fusion = bf16[64,1024]{1,0:T(8,128)(2,1)S(1)} fusion(bf16[4096,1024]{1,0:T(8,128)(2,1)} %slab_hbm.1, s32[1024]{0:T(1024)S(1)} %pad_clamp_fusion), kind=kCustom, calls=%fused_computation | custom fusion | bytes 262400 | tf_op jit(solution)/shard_map/jit(_take)/gather | solution.py:164
  15.3 2.1 %fusion.6 = f32[64,1024]{1,0:T(8,128)S(1)} fusion(bf16[64,1024]{1,0:T(8,128)(2,1)S(1)} %gather_fusion, bf16[1024,1024]{1,0:T(8,128)(2,1)} %gauss_hbm.1), kind=kOutput, calls=%fused_computation.22 | convolution fusion | flops 134217728 | bytes 2490368 | tf_op jit(solution)/shard_map/dot_general | solution.py:165
  17.4 1.5 %collective-permute-start = (f32[32,1024]{1,0:T(8,128)S(1)}, f32[32,1024]{1,0:T(8,128)S(1)}, u32[]{:S(2)}, u32[]{:S(2)}) collective-permute-start(f32[32,1024]{1,0:T(8,128)S(1)} %slice.11), channel_id=1, source_target_pairs={{0,1},{1,0},{2,3},{3,2},{4,5},{5,4},{6,7},{7,6},{8,9},{9,8},{10,11... | collective-permute-start | bytes 393224 | tf_op jit(solution)/shard_map/ppermute | solution.py:166
  18.9 1.0 collective-permute-done
  19.9 0.7 slice_add_fusion
  20.6 0.0 all-gather.2.cloned.1.call-update
  20.6 0.0 copy-start
  20.6 10.5 %shard_map.59 = (bf16[2048,1024]{1,0:T(8,128)(2,1)}, bf16[1024,1024]{1,0:T(8,128)(2,1)}) custom-call(bf16[4096,1024]{1,0:T(8,128)(2,1)} %slab_hbm.1, bf16[1024,1024]{1,0:T(8,128)(2,1)} %gauss_hbm.1), custom_call_target="tpu_custom_call" | custom-call | tf_op jit(solution)/shard_map/pallas_call | solution.py:134
  31.2 0.0 copy-done
  31.2 0.0 copy-start.1
  31.2 0.0 copy-start.2
  31.2 6.4 %fusion = f32[2048,1024]{1,0:T(8,128)S(1)} fusion(bf16[1024,1024]{1,0:T(8,128)(2,1)S(1)} %copy-done, bf16[4096,1024]{1,0:T(8,128)(2,1)} %slab_hbm.1, s32[]{:T(128)S(6)} %select_n.13), kind=kOutput, calls=%fused_computation.1 | convolution fusion | flops 4294967296 | bytes 14680068 | tf_op jit(solution)/shard_map/dot_general | solution.py:171
  37.6 0.0 copy-done.1
  37.7 0.0 copy-done.2
  37.7 6.7 %convolution_add_fusion.s_ref = f32[2048,1024]{1,0:T(8,128)} fusion(f32[2048,1024]{1,0:T(8,128)S(1)} %fusion, bf16[2048,1024]{1,0:T(8,128)(2,1)S(1)} %copy-done.1, bf16[1024,1024]{1,0:T(8,128)(2,1)S(1)} %copy-done.2), kind=kOutput, calls=%fused_computation.6 | convolution fusion | flops 4297064448 | bytes 23068672 | tf_op jit(solution)/shard_map/dot_general | solution.py:171
  44.4 59.3 %all-gather.2.cloned.1.call-done.slots_hbm = f32[4096,1024]{1,0:T(8,128)} async-done(((f32[32,1024]{1,0:T(8,128)}), f32[4096,1024]{1,0:T(8,128)}) %all-gather.2.cloned.1.call-update) | async-done | bytes 16777232 | tf_op jit(solution)/shard_map/all_gather | solution.py:167
  103.7 26.8 %shard_map.60 = (f32[2048,1024]{1,0:T(8,128)}, f32[8,1024]{1,0:T(8,128)}) custom-call(s32[1024]{0:T(1024)} %get-tuple-element.7.idx_ref, s32[1]{0:T(128)} %bitcast.own_ref, f32[2048,1024]{1,0:T(8,128)} %convolution_add_fusion.s_ref, f32[4096,1024]{1,0:T(8,128)} %all-gather.2.cloned.1.call-done.slots_hbm, f32[8,128,128]{2,1,0:T(8,128)} %b_ref.1), custom_call_target="tpu_custom_call" | custom-call | tf_op jit(solution)/shard_map/pallas_call | solution.py:80
  (7 shorter events, 0.0 us)
Async XLA Ops:
  7.2 96.5 %all-gather.2.cloned.1.call-start = ((), (), s32[]{:S(2)}) async-start(), calls=%async_computation | async-start | bytes 16908288 | tf_op jit(solution)/shard_map/all_gather | solution.py:167
  17.4 2.5 %collective-permute-start = (f32[32,1024]{1,0:T(8,128)S(1)}, f32[32,1024]{1,0:T(8,128)S(1)}, u32[]{:S(2)}, u32[]{:S(2)}) collective-permute-start(f32[32,1024]{1,0:T(8,128)S(1)} %slice.11), channel_id=1, source_target_pairs={{0,1},{1,0},{2,3},{3,2},{4,5},{5,4},{6,7},{7,6},{8,9},{9,8},{10,11... | collective-permute-start | bytes 393224 | tf_op jit(solution)/shard_map/ppermute | solution.py:166
  20.6 10.6 %copy-start = (bf16[1024,1024]{1,0:T(8,128)(2,1)S(1)}, bf16[1024,1024]{1,0:T(8,128)(2,1)}, u32[]{:S(2)}) copy-start(bf16[1024,1024]{1,0:T(8,128)(2,1)} %gauss_hbm.1) | copy-start | bytes 6291460
  31.2 6.5 %copy-start.1 = (bf16[2048,1024]{1,0:T(8,128)(2,1)S(1)}, bf16[2048,1024]{1,0:T(8,128)(2,1)}, u32[]{:S(2)}) copy-start(bf16[2048,1024]{1,0:T(8,128)(2,1)} %get-tuple-element.4) | copy-start | bytes 12582916
  31.2 6.5 %copy-start.2 = (bf16[1024,1024]{1,0:T(8,128)(2,1)S(1)}, bf16[1024,1024]{1,0:T(8,128)(2,1)}, u32[]{:S(2)}) copy-start(bf16[1024,1024]{1,0:T(8,128)(2,1)} %get-tuple-element.5) | copy-start | bytes 6291460
Sparse Core Ops, SparseCore 0:
  20.7 82.8 all-gather.1

commit v4 on v3

--- a/solution.py
+++ b/solution.py
@@ -17,6 +17,7 @@
     hi = x.astype(jnp.bfloat16)
     return hi, (x - hi.astype(jnp.float32)).astype(jnp.bfloat16)
 
+
 def dot3(a, b):
     a_hi, a_lo = split(a)
     b_hi, b_lo = split(b)
@@ -24,7 +25,48 @@
     return d(a_hi, b_hi) + (d(a_hi, b_lo) + d(a_lo, b_hi))
 
 
-def solve_kernel(factor, share, idx_ref, own_ref, s_ref, slots_hbm, b_ref, f_ref, piv_ref, pbuf, pcat, tcat, g, sem):
+def put3(dst, row0, hi, lo, rows):
+    dst[row0:row0 + rows] = hi
+    dst[row0 + rows:row0 + 2 * rows] = lo
+    dst[row0 + 2 * rows:row0 + 3 * rows] = hi
+
+
+def scale_kernel(s_ref, b_ref, o_ref, dcat):
+    nb = s_ref.shape[1] // BLK
+    pw = 2 * BLK
+
+    @pl.when(pl.program_id(0) == 0)
+    def _():
+        zero = jnp.zeros((BLK, BLK), jnp.float32)
+        for q in range(nb // 2):
+            a, b = 2 * q, 2 * q + 1
+            panel = jnp.concatenate(
+                [jnp.concatenate([b_ref[a], zero], axis=1), jnp.concatenate([zero, b_ref[b]], axis=1)], axis=0
+            )
+            hi, lo = split(panel)
+            put3(dcat.at[q], 0, hi, lo, pw)
+
+    for q in range(nb // 2):
+        cols = slice(q * pw, (q + 1) * pw)
+        a_hi, a_lo = split(s_ref[:, cols])
+        o_ref[:, cols] = jnp.dot(jnp.concatenate([a_hi, a_hi, a_lo], axis=1), dcat[q], preferred_element_type=jnp.float32)
+
+
+def scale(sketch, block_inverses):
+    rows, k = sketch.shape
+    full = lambda shape: pl.BlockSpec(shape, lambda i: (0,) * len(shape))
+    return pl.pallas_call(
+        scale_kernel,
+        out_shape=jax.ShapeDtypeStruct((rows, k), jnp.float32),
+        grid=(rows // TM,),
+        in_specs=[pl.BlockSpec((TM, k), lambda i: (i, 0)), full(block_inverses.shape)],
+        out_specs=pl.BlockSpec((TM, k), lambda i: (i, 0)),
+        scratch_shapes=[pltpu.VMEM((k // BLK // 2, 6 * BLK, 2 * BLK), jnp.bfloat16)],
+        compiler_params=pltpu.CompilerParams(vmem_limit_bytes=48 * 1024 * 1024),
+    )(sketch, block_inverses)
+
+
+def solve_kernel(factor, share, idx_ref, own_ref, s_ref, slots_hbm, b_ref, f_ref, piv_ref, pbuf, qcat, g, sem):
     nb = s_ref.shape[1] // BLK
     k = pbuf.shape[0]
     pw = 2 * BLK
@@ -38,44 +80,37 @@
         lax.fori_loop(0, k, fetch, 0, unroll=8)
         pltpu.make_async_copy(slots_hbm.at[pl.ds(0, k)], pbuf, sem).wait()
         piv_ref[...] = pbuf[pl.ds(pl.multiple_of(own_ref[0] * share, share), share), :]
-        for i in range(nb):
-            hi, lo = split(pbuf[i * BLK:(i + 1) * BLK, :] * factor)
-            pcat[3 * i * BLK:(3 * i + 1) * BLK, :] = hi
-            pcat[(3 * i + 1) * BLK:(3 * i + 2) * BLK, :] = lo
-            pcat[(3 * i + 2) * BLK:(3 * i + 3) * BLK, :] = hi
-        for q in range(nb // 2):
-            a, b = 2 * q, 2 * q + 1
-            cross = -dot3(dot3(b_ref[a], pbuf[a * BLK:b * BLK, b * BLK:(b + 1) * BLK] * factor), b_ref[b])
-            zero = jnp.zeros((BLK, BLK), jnp.float32)
-            panel = jnp.concatenate(
-                [jnp.concatenate([b_ref[a], cross], axis=1), jnp.concatenate([zero, b_ref[b]], axis=1)], axis=0
-            )
-            hi, lo = split(panel)
-            tcat[q, 0:pw, :] = hi
-            tcat[q, pw:2 * pw, :] = lo
-            tcat[q, 2 * pw:3 * pw, :] = hi
-
-    for q in range(nb // 2):
-        cols = slice(q * pw, (q + 1) * pw)
+        for j in range(1, nb):
+            q = dot3(pbuf[: j * BLK, j * BLK:(j + 1) * BLK] * factor, b_ref[j])
+            hi, lo = split(q)
+            for i in range(j):
+                put3(qcat.at[:, j * BLK:(j + 1) * BLK], 3 * i * BLK, hi[i * BLK:(i + 1) * BLK], lo[i * BLK:(i + 1) * BLK], BLK)
+
+    for p in range(nb // 2):
+        a, b = 2 * p, 2 * p + 1
+        cols = slice(p * pw, (p + 1) * pw)
         acc = s_ref[:, cols]
-        if q > 0:
-            acc = acc - jnp.dot(g[:, : 3 * q * pw], pcat[: 3 * q * pw, cols], preferred_element_type=jnp.float32)
-        a_hi, a_lo = split(acc)
-        out = jnp.dot(jnp.concatenate([a_hi, a_hi, a_lo], axis=1), tcat[q], preferred_element_type=jnp.float32)
-        f_ref[:, cols] = out
-        if q + 1 < nb // 2:
-            o_hi, o_lo = split(out)
-            for h in range(2):
-                blk = 2 * q + h
-                part = slice(h * BLK, (h + 1) * BLK)
-                g[:, 3 * blk * BLK:(3 * blk + 1) * BLK] = o_hi[:, part]
-                g[:, (3 * blk + 1) * BLK:(3 * blk + 2) * BLK] = o_hi[:, part]
-                g[:, (3 * blk + 2) * BLK:(3 * blk + 3) * BLK] = o_lo[:, part]
+        if p > 0:
+            acc = acc - jnp.dot(g[:, : 3 * p * pw], qcat[: 3 * p * pw, cols], preferred_element_type=jnp.float32)
+        f_a = acc[:, :BLK]
+        a_hi, a_lo = split(f_a)
+        f_b = acc[:, BLK:] - jnp.dot(
+            jnp.concatenate([a_hi, a_hi, a_lo], axis=1), qcat[3 * a * BLK:3 * b * BLK, b * BLK:(b + 1) * BLK], preferred_element_type=jnp.float32
+        )
+        f_ref[:, a * BLK:b * BLK] = f_a
+        f_ref[:, b * BLK:(b + 1) * BLK] = f_b
+        if p + 1 < nb // 2:
+            b_hi, b_lo = split(f_b)
+            g[:, 3 * a * BLK:(3 * a + 1) * BLK] = a_hi
+            g[:, (3 * a + 1) * BLK:(3 * a + 2) * BLK] = a_hi
+            g[:, (3 * a + 2) * BLK:(3 * a + 3) * BLK] = a_lo
+            g[:, 3 * b * BLK:(3 * b + 1) * BLK] = b_hi
+            g[:, (3 * b + 1) * BLK:(3 * b + 2) * BLK] = b_hi
+            g[:, (3 * b + 2) * BLK:(3 * b + 3) * BLK] = b_lo
 
 
 def solve(sketch, slots, idx, owner, share, block_inverses):
     rows, k = sketch.shape
-    nb = k // BLK
     full = lambda shape: pl.BlockSpec(shape, lambda i, *_: (0,) * len(shape))
     return pl.pallas_call(
         functools.partial(solve_kernel, 1.0 / k**0.5, share),
@@ -88,7 +123,6 @@
             scratch_shapes=[
                 pltpu.VMEM((k, k), jnp.float32),
                 pltpu.VMEM((3 * k, k), jnp.bfloat16),
-                pltpu.VMEM((nb // 2, 6 * BLK, 2 * BLK), jnp.bfloat16),
                 pltpu.VMEM((TM, 3 * k), jnp.bfloat16),
                 pltpu.SemaphoreType.DMA,
             ],
@@ -173,7 +207,8 @@
     )
 
     share = width // devices
-    factor_rows, own_pivots = solve(sketch, slots, block_of * SLOTS + rank, owner[None], share, block_inverses)
+    scaled = scale(sketch, block_inverses)
+    factor_rows, own_pivots = solve(scaled, slots, block_of * SLOTS + rank, owner[None], share, block_inverses)
     return (factor_rows, own_pivots)
 
 

time: 138 us -> 135 us (0.978)
  waiting for transfers between devices: 60.3 us -> 52.3 us
  Pallas kernels: 37.3 us -> 42.6 us
    all_gather x1, waiting for transfers between devices: 59.3 us -> 51.3 us  [on_device(): slots = lax.all_gather(own_slots, ('row', 'col'), tiled=True)]
    pallas_call x0 -> x1, Pallas kernels: none -> 7.86 us  [scale(): pl.pallas_call(scale_kernel, out_shape=jax.ShapeDtypeStruct((rows, k), jn...]
    pallas_call x1, Pallas kernels: 26.8 us -> 24.2 us  [solve(): pl.pallas_call(functools.partial(solve_kernel, 1.0 / k ** 0.5, share), ou...]
  transfers between devices with their start and end apart: 2 -> 2, of which waited for: 2 -> 2; matrix products, arithmetic and copies ran while one was open for 10% -> 10% of each run, Pallas kernels for 8% -> 14%
where the time goes in v4:
time: 135 us
  waiting for transfers between devices  52.3 us (39%)
  Pallas kernels  42.6 us (32%)
  matrix products  15.3 us (11%)
  between operations  14.2 us (11%)
  local copies, waits for them, and re-layouts  5.3 us (4%)
  other arithmetic  3.47 us (3%)
  starting transfers between devices  1.72 us (1%)
    all_gather x1, waiting for transfers between devices, on_device(): slots = lax.all_gather(own_slots, ('row', 'col'), tiled=True)  51.3 us
    pallas_call x1, Pallas kernels, solve(): pl.pallas_call(functools.partial(solve_kernel, 1.0 / k ** 0.5, share), ou...  24.2 us
    pallas_call x1, Pallas kernels, exchange(): pl.pallas_call(exchange_kernel, out_shape=(jax.ShapeDtypeStruct((rows, sl...  10.5 us
    pallas_call x1, Pallas kernels, scale(): pl.pallas_call(scale_kernel, out_shape=jax.ShapeDtypeStruct((rows, k), jn...  7.86 us
    dot_general x1, matrix products, on_device(): jnp.dot(other_slab, other_gauss, preferred_element_type=jnp.float32)  6.78 us
    dot_general x1, matrix products, on_device(): jnp.dot(mine, gauss, preferred_element_type=jnp.float32)  6.43 us
    gather x1, local copies, waits for them, and re-layouts, on_device(): rows = jnp.take(slab, where_row, axis=0, mode='clip')  5.26 us
  transfers between devices with their start and end apart: 2, of which 2 were waited for; matrix products, arithmetic and copies ran while one was open for 10% of the time, Pallas kernels for 14%

profile of v4, /device:TPU:1, one launch (start us, length us, event | category | flops | bytes accessed | tf_op | source)
XLA Modules:
  0.0 134.9 jit_solution(2102801865529238019)
XLA Ops:
  7.2 0.0 all-gather.2.cloned.1.call-start
  7.2 0.1 pad_add_fusion
  7.3 0.7 add_select_fusion
  8.0 0.5 convert_reduce_fusion
  8.5 1.3 multiply_subtract_fusion
  9.8 0.2 select_reduce_fusion
  10.1 5.3 %gather_fusion = bf16[64,1024]{1,0:T(8,128)(2,1)S(1)} fusion(bf16[4096,1024]{1,0:T(8,128)(2,1)} %slab_hbm.1, s32[1024]{0:T(1024)S(1)} %pad_clamp_fusion), kind=kCustom, calls=%fused_computation | custom fusion | bytes 262400 | tf_op jit(solution)/shard_map/jit(_take)/gather | solution.py:198
  15.3 2.1 %fusion.6 = f32[64,1024]{1,0:T(8,128)S(1)} fusion(bf16[64,1024]{1,0:T(8,128)(2,1)S(1)} %gather_fusion, bf16[1024,1024]{1,0:T(8,128)(2,1)} %gauss_hbm.1), kind=kOutput, calls=%fused_computation.22 | convolution fusion | flops 134217728 | bytes 2490368 | tf_op jit(solution)/shard_map/dot_general | solution.py:199
  17.4 1.7 %collective-permute-start = (f32[32,1024]{1,0:T(8,128)S(1)}, f32[32,1024]{1,0:T(8,128)S(1)}, u32[]{:S(2)}, u32[]{:S(2)}) collective-permute-start(f32[32,1024]{1,0:T(8,128)S(1)} %slice.11), channel_id=1, source_target_pairs={{0,1},{1,0},{2,3},{3,2},{4,5},{5,4},{6,7},{7,6},{8,9},{9,8},{10,11... | collective-permute-start | bytes 393224 | tf_op jit(solution)/shard_map/ppermute | solution.py:200
  19.1 1.0 collective-permute-done
  20.1 0.7 slice_add_fusion
  20.8 0.0 all-gather.2.cloned.1.call-update
  20.8 0.0 copy-start.1
  20.8 10.5 %shard_map.59 = (bf16[2048,1024]{1,0:T(8,128)(2,1)}, bf16[1024,1024]{1,0:T(8,128)(2,1)}) custom-call(bf16[4096,1024]{1,0:T(8,128)(2,1)} %slab_hbm.1, bf16[1024,1024]{1,0:T(8,128)(2,1)} %gauss_hbm.1), custom_call_target="tpu_custom_call" | custom-call | tf_op jit(solution)/shard_map/pallas_call | solution.py:168
  31.4 0.0 copy-done.1
  31.4 0.0 copy-start.2
  31.4 0.0 copy-start.3
  31.4 6.4 %fusion = f32[2048,1024]{1,0:T(8,128)S(1)} fusion(bf16[1024,1024]{1,0:T(8,128)(2,1)S(1)} %copy-done.1, bf16[4096,1024]{1,0:T(8,128)(2,1)} %slab_hbm.1, s32[]{:T(128)S(6)} %select_n.13), kind=kOutput, calls=%fused_computation.1 | convolution fusion | flops 4294967296 | bytes 14680068 | tf_op jit(solution)/shard_map/dot_general | solution.py:205
  37.8 0.0 copy-done.2
  37.8 0.0 copy-done.3
  37.9 0.0 copy-start
  37.9 6.8 %convolution_add_fusion.s_ref = f32[2048,1024]{1,0:T(8,128)} fusion(f32[2048,1024]{1,0:T(8,128)S(1)} %fusion, bf16[2048,1024]{1,0:T(8,128)(2,1)S(1)} %copy-done.2, bf16[1024,1024]{1,0:T(8,128)(2,1)S(1)} %copy-done.3), kind=kOutput, calls=%fused_computation.6 | convolution fusion | flops 4297064448 | bytes 23068672 | tf_op jit(solution)/shard_map/dot_general | solution.py:205
  44.6 0.0 copy-done
  44.6 7.9 %shard_map.60.s_ref = f32[2048,1024]{1,0:T(8,128)} custom-call(f32[2048,1024]{1,0:T(8,128)} %convolution_add_fusion.s_ref, f32[8,128,128]{2,1,0:T(8,128)S(1)} %copy-done), custom_call_target="tpu_custom_call" | custom-call | tf_op jit(solution)/shard_map/pallas_call | solution.py:58
  52.5 51.3 %all-gather.2.cloned.1.call-done.slots_hbm = f32[4096,1024]{1,0:T(8,128)} async-done(((f32[32,1024]{1,0:T(8,128)}), f32[4096,1024]{1,0:T(8,128)}) %all-gather.2.cloned.1.call-update) | async-done | bytes 16777232 | tf_op jit(solution)/shard_map/all_gather | solution.py:201
  103.8 24.2 %shard_map.61 = (f32[2048,1024]{1,0:T(8,128)}, f32[8,1024]{1,0:T(8,128)}) custom-call(s32[1024]{0:T(1024)} %get-tuple-element.7.idx_ref, s32[1]{0:T(128)} %bitcast.own_ref, f32[2048,1024]{1,0:T(8,128)} %shard_map.60.s_ref, f32[4096,1024]{1,0:T(8,128)} %all-gather.2.cloned.1.call-done.slots_hbm, f32[8,128,128]{2,1,0:T(8,128)} %b_ref.3), custom_call_target="tpu_custom_call" | custom-call | tf_op jit(solution)/shard_map/pallas_call | solution.py:115
  (7 shorter events, 0.0 us)
Async XLA Ops:
  7.2 96.7 %all-gather.2.cloned.1.call-start = ((), (), s32[]{:S(2)}) async-start(), calls=%async_computation | async-start | bytes 16908288 | tf_op jit(solution)/shard_map/all_gather | solution.py:201
  17.4 2.7 %collective-permute-start = (f32[32,1024]{1,0:T(8,128)S(1)}, f32[32,1024]{1,0:T(8,128)S(1)}, u32[]{:S(2)}, u32[]{:S(2)}) collective-permute-start(f32[32,1024]{1,0:T(8,128)S(1)} %slice.11), channel_id=1, source_target_pairs={{0,1},{1,0},{2,3},{3,2},{4,5},{5,4},{6,7},{7,6},{8,9},{9,8},{10,11... | collective-permute-start | bytes 393224 | tf_op jit(solution)/shard_map/ppermute | solution.py:200
  20.8 10.6 %copy-start.1 = (bf16[1024,1024]{1,0:T(8,128)(2,1)S(1)}, bf16[1024,1024]{1,0:T(8,128)(2,1)}, u32[]{:S(2)}) copy-start(bf16[1024,1024]{1,0:T(8,128)(2,1)} %gauss_hbm.1) | copy-start | bytes 6291460
  31.4 6.5 %copy-start.2 = (bf16[2048,1024]{1,0:T(8,128)(2,1)S(1)}, bf16[2048,1024]{1,0:T(8,128)(2,1)}, u32[]{:S(2)}) copy-start(bf16[2048,1024]{1,0:T(8,128)(2,1)} %get-tuple-element.4) | copy-start | bytes 12582916
  31.4 6.5 %copy-start.3 = (bf16[1024,1024]{1,0:T(8,128)(2,1)S(1)}, bf16[1024,1024]{1,0:T(8,128)(2,1)}, u32[]{:S(2)}) copy-start(bf16[1024,1024]{1,0:T(8,128)(2,1)} %get-tuple-element.5) | copy-start | bytes 6291460
  37.9 6.8 %copy-start = (f32[8,128,128]{2,1,0:T(8,128)S(1)}, f32[8,128,128]{2,1,0:T(8,128)}, u32[]{:S(2)}) copy-start(f32[8,128,128]{2,1,0:T(8,128)} %b_ref.3) | copy-start | bytes 1572868
Sparse Core Ops, SparseCore 0:
  20.9 82.8 all-gather.1

commit v5 on v4

--- a/solution.py
+++ b/solution.py
@@ -73,13 +73,18 @@
 
     @pl.when(pl.program_id(0) == 0)
     def _():
+        used = k - BLK
+
         def fetch(r, carry):
-            pltpu.make_async_copy(slots_hbm.at[pl.ds(idx_ref[r], 1)], pbuf.at[pl.ds(r, 1)], sem).start()
+            pltpu.make_async_copy(slots_hbm.at[pl.ds(idx_ref[r], 1)], pbuf.at[pl.ds(r, 1)], sem.at[0]).start()
             return carry
 
-        lax.fori_loop(0, k, fetch, 0, unroll=8)
-        pltpu.make_async_copy(slots_hbm.at[pl.ds(0, k)], pbuf, sem).wait()
-        piv_ref[...] = pbuf[pl.ds(pl.multiple_of(own_ref[0] * share, share), share), :]
+        lax.fori_loop(0, used, fetch, 0, unroll=8)
+        first = own_ref[0] * share
+        for r in range(share):
+            pltpu.make_async_copy(slots_hbm.at[pl.ds(idx_ref[first + r], 1)], piv_ref.at[pl.ds(r, 1)], sem.at[1]).start()
+        pltpu.make_async_copy(slots_hbm.at[pl.ds(0, used)], pbuf.at[pl.ds(0, used)], sem.at[0]).wait()
+        pltpu.make_async_copy(slots_hbm.at[pl.ds(0, share)], piv_ref, sem.at[1]).wait()
         for j in range(1, nb):
             q = dot3(pbuf[: j * BLK, j * BLK:(j + 1) * BLK] * factor, b_ref[j])
             hi, lo = split(q)
@@ -124,7 +129,7 @@
                 pltpu.VMEM((k, k), jnp.float32),
                 pltpu.VMEM((3 * k, k), jnp.bfloat16),
                 pltpu.VMEM((TM, 3 * k), jnp.bfloat16),
-                pltpu.SemaphoreType.DMA,
+                pltpu.SemaphoreType.DMA((2,)),
             ],
         ),
         compiler_params=pltpu.CompilerParams(vmem_limit_bytes=56 * 1024 * 1024),
@@ -195,7 +200,8 @@
     slot_ids = jnp.concatenate([jnp.arange(SLOTS), jnp.arange(SLOTS)])
     hit = (block_of[None, :] == targets[:, None]) & (rank[None, :] == slot_ids[:, None])
     where_row = jnp.sum(jnp.where(hit, local[None, :], 0), axis=1) + offsets
-    rows = jnp.take(slab, where_row, axis=0, mode="clip")
+    pick = where_row[:, None] == jnp.arange(slab.shape[0], dtype=jnp.int32)[None, :]
+    rows = jnp.dot(pick.astype(slab.dtype), slab, preferred_element_type=jnp.float32).astype(slab.dtype)
     parts = jnp.dot(rows, gauss, preferred_element_type=jnp.float32)
     own_slots = parts[:SLOTS] + lax.ppermute(parts[SLOTS:], "col", swap)
     slots = lax.all_gather(own_slots, ("row", "col"), tiled=True)

time: 135 us -> 133 us (0.985)
  local copies, waits for them, and re-layouts: 5.3 us -> 0.04 us
  matrix products: 15.3 us -> 19.2 us
    gather x1 -> x0, local copies, waits for them, and re-layouts: 5.26 us -> none  [on_device(): rows = jnp.take(slab, where_row, axis=0, mode='clip')]
    dot_general x1, matrix products: 2.07 us -> 5.96 us  [on_device(): parts = jnp.dot(rows, gauss, preferred_element_type=jnp.float32)]
where the time goes in v5:
time: 133 us
  waiting for transfers between devices  52.3 us (39%)
  Pallas kernels  42 us (32%)
  matrix products  19.2 us (14%)
  between operations  14.2 us (11%)
  other arithmetic  3.47 us (3%)
  starting transfers between devices  1.72 us (1%)
    all_gather x1, waiting for transfers between devices, on_device(): slots = lax.all_gather(own_slots, ('row', 'col'), tiled=True)  51.3 us
    pallas_call x1, Pallas kernels, solve(): pl.pallas_call(functools.partial(solve_kernel, 1.0 / k ** 0.5, share), ou...  23.6 us
    pallas_call x1, Pallas kernels, exchange(): pl.pallas_call(exchange_kernel, out_shape=(jax.ShapeDtypeStruct((rows, sl...  10.5 us
    pallas_call x1, Pallas kernels, scale(): pl.pallas_call(scale_kernel, out_shape=jax.ShapeDtypeStruct((rows, k), jn...  7.86 us
    dot_general x1, matrix products, on_device(): jnp.dot(other_slab, other_gauss, preferred_element_type=jnp.float32)  6.78 us
    dot_general x1, matrix products, on_device(): jnp.dot(mine, gauss, preferred_element_type=jnp.float32)  6.44 us
    dot_general x1, matrix products, on_device(): parts = jnp.dot(rows, gauss, preferred_element_type=jnp.float32)  5.96 us
  transfers between devices with their start and end apart: 2, of which 2 were waited for; matrix products, arithmetic and copies ran while one was open for 10% of the time, Pallas kernels for 14%

profile of v5, /device:TPU:1, one launch (start us, length us, event | category | flops | bytes accessed | tf_op | source)
XLA Modules:
  0.0 132.9 jit_solution(6371666338784884229)
XLA Ops:
  7.2 0.0 all-gather.2.cloned.1.call-start
  7.2 0.1 pad_add_fusion
  7.3 0.7 add_select_fusion
  8.0 0.5 convert_reduce_fusion
  8.5 1.3 multiply_subtract_fusion
  9.8 0.2 select_reduce_fusion
  10.1 6.0 %fusion.3 = f32[64,1024]{1,0:T(8,128)S(1)} fusion(bf16[1024,1024]{1,0:T(8,128)(2,1)} %gauss_hbm.1, bf16[4096,1024]{1,0:T(8,128)(2,1)} %slab_hbm.1, s32[64]{0:T(128)S(1)} %multiply_add_fusion.1), kind=kOutput, calls=%fused_computation.7 | convolution fusion | flops 671416320 | bytes 10748160 | tf_op jit(solution)/shard_map/dot_general | solution.py:205
  16.0 1.7 %collective-permute-start = (f32[32,1024]{1,0:T(8,128)S(1)}, f32[32,1024]{1,0:T(8,128)S(1)}, u32[]{:S(2)}, u32[]{:S(2)}) collective-permute-start(f32[32,1024]{1,0:T(8,128)S(1)} %slice.9), channel_id=1, source_target_pairs={{0,1},{1,0},{2,3},{3,2},{4,5},{5,4},{6,7},{7,6},{8,9},{9,8},{10,11... | collective-permute-start | bytes 393224 | tf_op jit(solution)/shard_map/ppermute | solution.py:206
  17.7 1.0 collective-permute-done
  18.7 0.7 slice_add_fusion
  19.4 0.0 all-gather.2.cloned.1.call-update
  19.4 0.0 copy-start.1
  19.4 10.5 %shard_map.59 = (bf16[2048,1024]{1,0:T(8,128)(2,1)}, bf16[1024,1024]{1,0:T(8,128)(2,1)}) custom-call(bf16[4096,1024]{1,0:T(8,128)(2,1)} %slab_hbm.1, bf16[1024,1024]{1,0:T(8,128)(2,1)} %gauss_hbm.1), custom_call_target="tpu_custom_call" | custom-call | tf_op jit(solution)/shard_map/pallas_call | solution.py:173
  30.0 0.0 copy-done.1
  30.0 0.0 copy-start.2
  30.0 0.0 copy-start.3
  30.0 6.4 %fusion = f32[2048,1024]{1,0:T(8,128)S(1)} fusion(bf16[1024,1024]{1,0:T(8,128)(2,1)S(1)} %copy-done.1, bf16[4096,1024]{1,0:T(8,128)(2,1)} %slab_hbm.1, s32[]{:T(128)S(6)} %select_n.13), kind=kOutput, calls=%fused_computation | convolution fusion | flops 4294967296 | bytes 14680068 | tf_op jit(solution)/shard_map/dot_general | solution.py:211
  36.5 0.0 copy-done.2
  36.5 0.0 copy-done.3
  36.5 0.0 copy-start
  36.5 6.8 %convolution_add_fusion.s_ref = f32[2048,1024]{1,0:T(8,128)} fusion(f32[2048,1024]{1,0:T(8,128)S(1)} %fusion, bf16[2048,1024]{1,0:T(8,128)(2,1)S(1)} %copy-done.2, bf16[1024,1024]{1,0:T(8,128)(2,1)S(1)} %copy-done.3), kind=kOutput, calls=%fused_computation.5 | convolution fusion | flops 4297064448 | bytes 23068672 | tf_op jit(solution)/shard_map/dot_general | solution.py:211
  43.3 0.0 copy-done
  43.3 7.9 %shard_map.60.s_ref = f32[2048,1024]{1,0:T(8,128)} custom-call(f32[2048,1024]{1,0:T(8,128)} %convolution_add_fusion.s_ref, f32[8,128,128]{2,1,0:T(8,128)S(1)} %copy-done), custom_call_target="tpu_custom_call" | custom-call | tf_op jit(solution)/shard_map/pallas_call | solution.py:58
  51.1 51.3 %all-gather.2.cloned.1.call-done.slots_hbm = f32[4096,1024]{1,0:T(8,128)} async-done(((f32[32,1024]{1,0:T(8,128)}), f32[4096,1024]{1,0:T(8,128)}) %all-gather.2.cloned.1.call-update) | async-done | bytes 16777232 | tf_op jit(solution)/shard_map/all_gather | solution.py:207
  102.5 23.6 %shard_map.61 = (f32[2048,1024]{1,0:T(8,128)}, f32[8,1024]{1,0:T(8,128)}) custom-call(s32[1024]{0:T(1024)} %get-tuple-element.7.idx_ref, s32[1]{0:T(128)} %bitcast.own_ref, f32[2048,1024]{1,0:T(8,128)} %shard_map.60.s_ref, f32[4096,1024]{1,0:T(8,128)} %all-gather.2.cloned.1.call-done.slots_hbm, f32[8,128,128]{2,1,0:T(8,128)} %b_ref.3), custom_call_target="tpu_custom_call" | custom-call | tf_op jit(solution)/shard_map/pallas_call | solution.py:120
  (6 shorter events, 0.0 us)
Async XLA Ops:
  7.2 95.3 %all-gather.2.cloned.1.call-start = ((), (), s32[]{:S(2)}) async-start(), calls=%async_computation | async-start | bytes 16908288 | tf_op jit(solution)/shard_map/all_gather | solution.py:207
  16.0 2.7 %collective-permute-start = (f32[32,1024]{1,0:T(8,128)S(1)}, f32[32,1024]{1,0:T(8,128)S(1)}, u32[]{:S(2)}, u32[]{:S(2)}) collective-permute-start(f32[32,1024]{1,0:T(8,128)S(1)} %slice.9), channel_id=1, source_target_pairs={{0,1},{1,0},{2,3},{3,2},{4,5},{5,4},{6,7},{7,6},{8,9},{9,8},{10,11... | collective-permute-start | bytes 393224 | tf_op jit(solution)/shard_map/ppermute | solution.py:206
  19.4 10.6 %copy-start.1 = (bf16[1024,1024]{1,0:T(8,128)(2,1)S(1)}, bf16[1024,1024]{1,0:T(8,128)(2,1)}, u32[]{:S(2)}) copy-start(bf16[1024,1024]{1,0:T(8,128)(2,1)} %gauss_hbm.1) | copy-start | bytes 6291460
  30.0 6.5 %copy-start.2 = (bf16[2048,1024]{1,0:T(8,128)(2,1)S(1)}, bf16[2048,1024]{1,0:T(8,128)(2,1)}, u32[]{:S(2)}) copy-start(bf16[2048,1024]{1,0:T(8,128)(2,1)} %get-tuple-element.4) | copy-start | bytes 12582916
  30.0 6.5 %copy-start.3 = (bf16[1024,1024]{1,0:T(8,128)(2,1)S(1)}, bf16[1024,1024]{1,0:T(8,128)(2,1)}, u32[]{:S(2)}) copy-start(bf16[1024,1024]{1,0:T(8,128)(2,1)} %get-tuple-element.5) | copy-start | bytes 6291460
  36.5 6.8 %copy-start = (f32[8,128,128]{2,1,0:T(8,128)S(1)}, f32[8,128,128]{2,1,0:T(8,128)}, u32[]{:S(2)}) copy-start(f32[8,128,128]{2,1,0:T(8,128)} %b_ref.3) | copy-start | bytes 1572868
Sparse Core Ops, SparseCore 0:
  19.5 82.8 all-gather.1

commit v6 on v5

--- a/solution.py
+++ b/solution.py
@@ -10,6 +10,7 @@
 K = 1024
 BLK = 128
 SLOTS = 32
+GROUP = 16
 TM = 1024
 
 
@@ -134,6 +135,33 @@
         ),
         compiler_params=pltpu.CompilerParams(vmem_limit_bytes=56 * 1024 * 1024),
     )(idx, owner, sketch, slots, block_inverses)
+
+
+def pick_kernel(base_ref, within_ref, slab_hbm, gauss_hbm, out_ref, grp, gbuf, sems):
+    n = within_ref.shape[0]
+    load_gauss = pltpu.make_async_copy(gauss_hbm, gbuf, sems.at[0])
+    load_gauss.start()
+    for s in range(n):
+        start = pl.multiple_of(base_ref[s] * GROUP, GROUP)
+        pltpu.make_async_copy(slab_hbm.at[pl.ds(start, GROUP)], grp.at[pl.ds(s * GROUP, GROUP)], sems.at[1]).start()
+    pltpu.make_async_copy(slab_hbm.at[pl.ds(0, n * GROUP)], grp, sems.at[1]).wait()
+    target = lax.broadcasted_iota(jnp.int32, (n, n * GROUP), 0) * GROUP + within_ref[...]
+    onehot = (lax.broadcasted_iota(jnp.int32, (n, n * GROUP), 1) == target).astype(grp.dtype)
+    rows = jnp.dot(onehot, grp[...], preferred_element_type=jnp.float32).astype(grp.dtype)
+    load_gauss.wait()
+    out_ref[...] = jnp.dot(rows, gbuf[...], preferred_element_type=jnp.float32)
+
+
+def pick(slab, gauss, where_row):
+    n = where_row.shape[0]
+    anywhere = pl.BlockSpec(memory_space=pl.ANY)
+    return pl.pallas_call(
+        pick_kernel,
+        out_shape=jax.ShapeDtypeStruct((n, gauss.shape[1]), jnp.float32),
+        in_specs=[pl.BlockSpec(memory_space=pltpu.SMEM), pl.BlockSpec(memory_space=pltpu.VMEM), anywhere, anywhere],
+        out_specs=pl.BlockSpec(memory_space=pltpu.VMEM),
+        scratch_shapes=[pltpu.VMEM((n * GROUP, slab.shape[1]), slab.dtype), pltpu.VMEM(gauss.shape, gauss.dtype), pltpu.SemaphoreType.DMA((2,))],
+    )(where_row // GROUP, (where_row % GROUP)[:, None], slab, gauss)
 
 
 def exchange_kernel(slab_hbm, gauss_hbm, slab_out, gauss_out, sems):
@@ -200,9 +228,7 @@
     slot_ids = jnp.concatenate([jnp.arange(SLOTS), jnp.arange(SLOTS)])
     hit = (block_of[None, :] == targets[:, None]) & (rank[None, :] == slot_ids[:, None])
     where_row = jnp.sum(jnp.where(hit, local[None, :], 0), axis=1) + offsets
-    pick = where_row[:, None] == jnp.arange(slab.shape[0], dtype=jnp.int32)[None, :]
-    rows = jnp.dot(pick.astype(slab.dtype), slab, preferred_element_type=jnp.float32).astype(slab.dtype)
-    parts = jnp.dot(rows, gauss, preferred_element_type=jnp.float32)
+    parts = pick(slab, gauss, where_row)
     own_slots = parts[:SLOTS] + lax.ppermute(parts[SLOTS:], "col", swap)
     slots = lax.all_gather(own_slots, ("row", "col"), tiled=True)
 

time: 133 us -> 135 us (1.015)
  matrix products: 19.2 us -> 13.2 us
  Pallas kernels: 42 us -> 47 us
  local copies, waits for them, and re-layouts: 0.04 us -> 1.66 us
  other arithmetic: 3.47 us -> 4.88 us
    dot_general x1 -> x0, matrix products: 5.96 us -> none  [on_device(): parts = jnp.dot(rows, gauss, preferred_element_type=jnp.float32)]
    pallas_call x0 -> x1, Pallas kernels: none -> 5.07 us  [pick(): pl.pallas_call(pick_kernel, out_shape=jax.ShapeDtypeStruct((n, gauss.shap...]
where the time goes in v6:
time: 135 us
  waiting for transfers between devices  52.3 us (39%)
  Pallas kernels  47 us (35%)
  between operations  14.2 us (11%)
  matrix products  13.2 us (10%)
  other arithmetic  4.88 us (4%)
  local copies, waits for them, and re-layouts  1.66 us (1%)
  starting transfers between devices  1.61 us (1%)
    all_gather x1, waiting for transfers between devices, on_device(): slots = lax.all_gather(own_slots, ('row', 'col'), tiled=True)  51.3 us
    pallas_call x1, Pallas kernels, solve(): pl.pallas_call(functools.partial(solve_kernel, 1.0 / k ** 0.5, share), ou...  23.6 us
    pallas_call x1, Pallas kernels, exchange(): pl.pallas_call(exchange_kernel, out_shape=(jax.ShapeDtypeStruct((rows, sl...  10.5 us
    pallas_call x1, Pallas kernels, scale(): pl.pallas_call(scale_kernel, out_shape=jax.ShapeDtypeStruct((rows, k), jn...  7.88 us
    dot_general x1, matrix products, on_device(): jnp.dot(other_slab, other_gauss, preferred_element_type=jnp.float32)  6.78 us
    dot_general x1, matrix products, on_device(): jnp.dot(mine, gauss, preferred_element_type=jnp.float32)  6.43 us
    pallas_call x1, Pallas kernels, pick(): pl.pallas_call(pick_kernel, out_shape=jax.ShapeDtypeStruct((n, gauss.shap...  5.07 us
  transfers between devices with their start and end apart: 2, of which 2 were waited for; matrix products, arithmetic and copies ran while one was open for 10% of the time, Pallas kernels for 14%

profile of v6, /device:TPU:1, one launch (start us, length us, event | category | flops | bytes accessed | tf_op | source)
XLA Modules:
  0.0 134.9 jit_solution(11613593531531772764)
XLA Ops:
  7.2 0.0 all-gather.2.cloned.1.call-start
  7.2 0.1 pad_add_fusion
  7.3 0.7 add_select_fusion
  8.0 0.5 convert_reduce_fusion
  8.5 1.3 multiply_subtract_fusion
  9.8 0.2 select_reduce_fusion
  10.1 0.5 and_select_fusion.1.base_ref
  10.6 0.7 copy.7.within_ref
  11.3 5.1 %shard_map.61 = f32[64,1024]{1,0:T(8,128)} custom-call(s32[64]{0:T(128)} %and_select_fusion.1.base_ref, s32[64,1]{1,0:T(8,128)} %copy.7.within_ref, bf16[4096,1024]{1,0:T(8,128)(2,1)} %slab_hbm.3, bf16[1024,1024]{1,0:T(8,128)(2,1)} %gauss_hbm.3), custom_call_target="tpu_custom_call" | custom-call | tf_op jit(solution)/shard_map/pallas_call | solution.py:158
  16.4 0.9 slice.9
  17.3 1.6 %collective-permute-start = (f32[32,1024]{1,0:T(8,128)S(1)}, f32[32,1024]{1,0:T(8,128)S(1)}, u32[]{:S(2)}, u32[]{:S(2)}) collective-permute-start(f32[32,1024]{1,0:T(8,128)S(1)} %slice.9), channel_id=1, source_target_pairs={{0,1},{1,0},{2,3},{3,2},{4,5},{5,4},{6,7},{7,6},{8,9},{9,8},{10,11... | collective-permute-start | bytes 393224 | tf_op jit(solution)/shard_map/ppermute | solution.py:232
  18.9 1.0 collective-permute-done
  19.8 1.6 %slice_add_fusion = f32[32,1024]{1,0:T(8,128)} fusion(f32[32,1024]{1,0:T(8,128)S(1)} %collective-permute-done, f32[64,1024]{1,0:T(8,128)} %shard_map.61), kind=kLoop, calls=%fused_computation.7 | loop fusion | flops 32768 | bytes 393216 | tf_op jit(solution)/shard_map/add | solution.py:232
  21.4 0.0 all-gather.2.cloned.1.call-update
  21.4 0.0 copy-start.1
  21.4 10.5 %shard_map.59 = (bf16[2048,1024]{1,0:T(8,128)(2,1)}, bf16[1024,1024]{1,0:T(8,128)(2,1)}) custom-call(bf16[4096,1024]{1,0:T(8,128)(2,1)} %slab_hbm.3, bf16[1024,1024]{1,0:T(8,128)(2,1)} %gauss_hbm.3), custom_call_target="tpu_custom_call" | custom-call | tf_op jit(solution)/shard_map/pallas_call | solution.py:201
  32.0 0.0 copy-done.1
  32.0 0.0 copy-start.2
  32.0 0.0 copy-start.3
  32.0 6.4 %fusion = f32[2048,1024]{1,0:T(8,128)S(1)} fusion(bf16[1024,1024]{1,0:T(8,128)(2,1)S(1)} %copy-done.1, bf16[4096,1024]{1,0:T(8,128)(2,1)} %slab_hbm.3, s32[]{:T(128)S(6)} %select_n.25), kind=kOutput, calls=%fused_computation | convolution fusion | flops 4294967296 | bytes 14680068 | tf_op jit(solution)/shard_map/dot_general | solution.py:237
  38.5 0.0 copy-done.2
  38.5 0.0 copy-done.3
  38.5 0.0 copy-start
  38.5 6.8 %convolution_add_fusion.s_ref = f32[2048,1024]{1,0:T(8,128)} fusion(f32[2048,1024]{1,0:T(8,128)S(1)} %fusion, bf16[2048,1024]{1,0:T(8,128)(2,1)S(1)} %copy-done.2, bf16[1024,1024]{1,0:T(8,128)(2,1)S(1)} %copy-done.3), kind=kOutput, calls=%fused_computation.5 | convolution fusion | flops 4297064448 | bytes 23068672 | tf_op jit(solution)/shard_map/dot_general | solution.py:237
  45.3 0.0 copy-done
  45.3 7.9 %shard_map.60.s_ref = f32[2048,1024]{1,0:T(8,128)} custom-call(f32[2048,1024]{1,0:T(8,128)} %convolution_add_fusion.s_ref, f32[8,128,128]{2,1,0:T(8,128)S(1)} %copy-done), custom_call_target="tpu_custom_call" | custom-call | tf_op jit(solution)/shard_map/pallas_call | solution.py:59
  53.2 51.3 %all-gather.2.cloned.1.call-done.slots_hbm = f32[4096,1024]{1,0:T(8,128)} async-done(((f32[32,1024]{1,0:T(8,128)}), f32[4096,1024]{1,0:T(8,128)}) %all-gather.2.cloned.1.call-update) | async-done | bytes 16777232 | tf_op jit(solution)/shard_map/all_gather | solution.py:233
  104.4 23.6 %shard_map.62 = (f32[2048,1024]{1,0:T(8,128)}, f32[8,1024]{1,0:T(8,128)}) custom-call(s32[1024]{0:T(1024)} %get-tuple-element.9.idx_ref, s32[1]{0:T(128)} %bitcast.own_ref, f32[2048,1024]{1,0:T(8,128)} %shard_map.60.s_ref, f32[4096,1024]{1,0:T(8,128)} %all-gather.2.cloned.1.call-done.slots_hbm, f32[8,128,128]{2,1,0:T(8,128)} %b_ref.3), custom_call_target="tpu_custom_call" | custom-call | tf_op jit(solution)/shard_map/pallas_call | solution.py:121
  (5 shorter events, 0.0 us)
Async XLA Ops:
  7.2 97.3 %all-gather.2.cloned.1.call-start = ((), (), s32[]{:S(2)}) async-start(), calls=%async_computation | async-start | bytes 16908288 | tf_op jit(solution)/shard_map/all_gather | solution.py:233
  17.3 2.6 %collective-permute-start = (f32[32,1024]{1,0:T(8,128)S(1)}, f32[32,1024]{1,0:T(8,128)S(1)}, u32[]{:S(2)}, u32[]{:S(2)}) collective-permute-start(f32[32,1024]{1,0:T(8,128)S(1)} %slice.9), channel_id=1, source_target_pairs={{0,1},{1,0},{2,3},{3,2},{4,5},{5,4},{6,7},{7,6},{8,9},{9,8},{10,11... | collective-permute-start | bytes 393224 | tf_op jit(solution)/shard_map/ppermute | solution.py:232
  21.4 10.6 %copy-start.1 = (bf16[1024,1024]{1,0:T(8,128)(2,1)S(1)}, bf16[1024,1024]{1,0:T(8,128)(2,1)}, u32[]{:S(2)}) copy-start(bf16[1024,1024]{1,0:T(8,128)(2,1)} %gauss_hbm.3) | copy-start | bytes 6291460
  32.0 6.5 %copy-start.2 = (bf16[2048,1024]{1,0:T(8,128)(2,1)S(1)}, bf16[2048,1024]{1,0:T(8,128)(2,1)}, u32[]{:S(2)}) copy-start(bf16[2048,1024]{1,0:T(8,128)(2,1)} %get-tuple-element.4) | copy-start | bytes 12582916
  32.0 6.5 %copy-start.3 = (bf16[1024,1024]{1,0:T(8,128)(2,1)S(1)}, bf16[1024,1024]{1,0:T(8,128)(2,1)}, u32[]{:S(2)}) copy-start(bf16[1024,1024]{1,0:T(8,128)(2,1)} %get-tuple-element.5) | copy-start | bytes 6291460
  38.5 6.8 %copy-start = (f32[8,128,128]{2,1,0:T(8,128)S(1)}, f32[8,128,128]{2,1,0:T(8,128)}, u32[]{:S(2)}) copy-start(f32[8,128,128]{2,1,0:T(8,128)} %b_ref.3) | copy-start | bytes 1572868
Sparse Core Ops, SparseCore 0:
  21.5 82.8 all-gather.1

commit v7 on v5

--- a/solution.py
+++ b/solution.py
@@ -66,7 +66,7 @@
     )(sketch, block_inverses)
 
 
-def solve_kernel(factor, share, idx_ref, own_ref, s_ref, slots_hbm, b_ref, f_ref, piv_ref, pbuf, qcat, g, sem):
+def solve_kernel(factor, share, idx_ref, own_ref, s_ref, slots_hbm, b_ref, f_ref, piv_ref, pbuf, pown, qcat, g, sem):
     nb = s_ref.shape[1] // BLK
     k = pbuf.shape[0]
     pw = 2 * BLK
@@ -82,11 +82,12 @@
         lax.fori_loop(0, used, fetch, 0, unroll=8)
         first = own_ref[0] * share
         for r in range(share):
-            pltpu.make_async_copy(slots_hbm.at[pl.ds(idx_ref[first + r], 1)], piv_ref.at[pl.ds(r, 1)], sem.at[1]).start()
+            pltpu.make_async_copy(slots_hbm.at[pl.ds(idx_ref[first + r], 1)], pown.at[pl.ds(r, 1)], sem.at[1]).start()
         pltpu.make_async_copy(slots_hbm.at[pl.ds(0, used)], pbuf.at[pl.ds(0, used)], sem.at[0]).wait()
-        pltpu.make_async_copy(slots_hbm.at[pl.ds(0, share)], piv_ref, sem.at[1]).wait()
+        pltpu.make_async_copy(slots_hbm.at[pl.ds(0, share)], pown, sem.at[1]).wait()
+        piv_ref[...] = jnp.concatenate([pown[:, c, :] for c in range(nb)], axis=1)
         for j in range(1, nb):
-            q = dot3(pbuf[: j * BLK, j * BLK:(j + 1) * BLK] * factor, b_ref[j])
+            q = dot3(pbuf[: j * BLK, j, :] * factor, b_ref[j])
             hi, lo = split(q)
             for i in range(j):
                 put3(qcat.at[:, j * BLK:(j + 1) * BLK], 3 * i * BLK, hi[i * BLK:(i + 1) * BLK], lo[i * BLK:(i + 1) * BLK], BLK)
@@ -126,7 +127,8 @@
             in_specs=[pl.BlockSpec((TM, k), lambda i, *_: (i, 0)), pl.BlockSpec(memory_space=pl.ANY), full(block_inverses.shape)],
             out_specs=[pl.BlockSpec((TM, k), lambda i, *_: (i, 0)), full((share, k))],
             scratch_shapes=[
-                pltpu.VMEM((k, k), jnp.float32),
+                pltpu.VMEM((k, k // BLK, BLK), jnp.float32),
+                pltpu.VMEM((share, k // BLK, BLK), jnp.float32),
                 pltpu.VMEM((3 * k, k), jnp.bfloat16),
                 pltpu.VMEM((TM, 3 * k), jnp.bfloat16),
                 pltpu.SemaphoreType.DMA((2,)),
@@ -204,7 +206,7 @@
     rows = jnp.dot(pick.astype(slab.dtype), slab, preferred_element_type=jnp.float32).astype(slab.dtype)
     parts = jnp.dot(rows, gauss, preferred_element_type=jnp.float32)
     own_slots = parts[:SLOTS] + lax.ppermute(parts[SLOTS:], "col", swap)
-    slots = lax.all_gather(own_slots, ("row", "col"), tiled=True)
+    slots = lax.all_gather(own_slots.reshape(SLOTS, width // BLK, BLK), ("row", "col"), tiled=True)
 
     mine = lax.dynamic_slice_in_dim(slab, col * shard_rows, shard_rows, 0)
     other_slab, other_gauss = exchange(slab, gauss, shard_rows)

time: 133 us -> 136 us (1.023)
  Pallas kernels: 42 us -> 45.4 us
    pallas_call x1, Pallas kernels: 23.6 us -> 27 us  [solve(): pl.pallas_call(functools.partial(solve_kernel, 1.0 / k ** 0.5, share), ou...]
where the time goes in v7:
time: 136 us
  waiting for transfers between devices  52.3 us (38%)
  Pallas kernels  45.4 us (33%)
  matrix products  19.2 us (14%)
  between operations  14.2 us (10%)
  other arithmetic  2.82 us (2%)
  starting transfers between devices  1.54 us (1%)
    all_gather x1, waiting for transfers between devices, on_device(): lax.all_gather(own_slots.reshape(SLOTS, width // BLK, BLK), ('row', 'col'...  51.3 us
    pallas_call x1, Pallas kernels, solve(): pl.pallas_call(functools.partial(solve_kernel, 1.0 / k ** 0.5, share), ou...  27 us
    pallas_call x1, Pallas kernels, exchange(): pl.pallas_call(exchange_kernel, out_shape=(jax.ShapeDtypeStruct((rows, sl...  10.5 us
    pallas_call x1, Pallas kernels, scale(): pl.pallas_call(scale_kernel, out_shape=jax.ShapeDtypeStruct((rows, k), jn...  7.86 us
    dot_general x1, matrix products, on_device(): jnp.dot(other_slab, other_gauss, preferred_element_type=jnp.float32)  6.78 us
    dot_general x1, matrix products, on_device(): jnp.dot(mine, gauss, preferred_element_type=jnp.float32)  6.44 us
    dot_general x1, matrix products, on_device(): parts = jnp.dot(rows, gauss, preferred_element_type=jnp.float32)  5.96 us
  transfers between devices with their start and end apart: 2, of which 2 were waited for; matrix products, arithmetic and copies ran while one was open for 10% of the time, Pallas kernels for 14%

profile of v7, /device:TPU:1, one launch (start us, length us, event | category | flops | bytes accessed | tf_op | source)
XLA Modules:
  0.0 136.2 jit_solution(11431801962723687191)
XLA Ops:
  7.2 0.0 all-gather.2.cloned.1.call-start
  7.2 0.1 pad_add_fusion
  7.3 0.7 add_select_fusion
  8.0 0.5 convert_reduce_fusion
  8.5 1.3 multiply_subtract_fusion
  9.8 0.2 select_reduce_fusion
  10.1 6.0 %fusion.3 = f32[64,1024]{1,0:T(8,128)S(1)} fusion(bf16[1024,1024]{1,0:T(8,128)(2,1)} %gauss_hbm.1, bf16[4096,1024]{1,0:T(8,128)(2,1)} %slab_hbm.1, s32[64]{0:T(128)S(1)} %multiply_add_fusion.1), kind=kOutput, calls=%fused_computation.7 | convolution fusion | flops 671416320 | bytes 10748160 | tf_op jit(solution)/shard_map/dot_general | solution.py:207
  16.0 1.5 %collective-permute-start = (f32[32,1024]{1,0:T(8,128)S(1)}, f32[32,1024]{1,0:T(8,128)S(1)}, u32[]{:S(2)}, u32[]{:S(2)}) collective-permute-start(f32[32,1024]{1,0:T(8,128)S(1)} %slice.9), channel_id=1, source_target_pairs={{0,1},{1,0},{2,3},{3,2},{4,5},{5,4},{6,7},{7,6},{8,9},{9,8},{10,11... | collective-permute-start | bytes 393224 | tf_op jit(solution)/shard_map/ppermute | solution.py:208
  17.5 1.0 collective-permute-done
  18.6 0.7 copy.6
  19.2 0.0 all-gather.2.cloned.1.call-update
  19.3 0.0 copy-start.1
  19.3 10.5 %shard_map.59 = (bf16[2048,1024]{1,0:T(8,128)(2,1)}, bf16[1024,1024]{1,0:T(8,128)(2,1)}) custom-call(bf16[4096,1024]{1,0:T(8,128)(2,1)} %slab_hbm.1, bf16[1024,1024]{1,0:T(8,128)(2,1)} %gauss_hbm.1), custom_call_target="tpu_custom_call" | custom-call | tf_op jit(solution)/shard_map/pallas_call | solution.py:175
  29.8 0.0 copy-done.1
  29.8 0.0 copy-start.2
  29.9 0.0 copy-start.3
  29.9 6.4 %fusion = f32[2048,1024]{1,0:T(8,128)S(1)} fusion(bf16[1024,1024]{1,0:T(8,128)(2,1)S(1)} %copy-done.1, bf16[4096,1024]{1,0:T(8,128)(2,1)} %slab_hbm.1, s32[]{:T(128)S(6)} %select_n.13), kind=kOutput, calls=%fused_computation | convolution fusion | flops 4294967296 | bytes 14680068 | tf_op jit(solution)/shard_map/dot_general | solution.py:213
  36.3 0.0 copy-done.2
  36.3 0.0 copy-done.3
  36.3 0.0 copy-start
  36.3 6.8 %convolution_add_fusion.s_ref = f32[2048,1024]{1,0:T(8,128)} fusion(f32[2048,1024]{1,0:T(8,128)S(1)} %fusion, bf16[2048,1024]{1,0:T(8,128)(2,1)S(1)} %copy-done.2, bf16[1024,1024]{1,0:T(8,128)(2,1)S(1)} %copy-done.3), kind=kOutput, calls=%fused_computation.5 | convolution fusion | flops 4297064448 | bytes 23068672 | tf_op jit(solution)/shard_map/dot_general | solution.py:213
  43.1 0.0 copy-done
  43.1 7.9 %shard_map.60.s_ref = f32[2048,1024]{1,0:T(8,128)} custom-call(f32[2048,1024]{1,0:T(8,128)} %convolution_add_fusion.s_ref, f32[8,128,128]{2,1,0:T(8,128)S(1)} %copy-done), custom_call_target="tpu_custom_call" | custom-call | tf_op jit(solution)/shard_map/pallas_call | solution.py:58
  51.0 51.3 %all-gather.2.cloned.1.call-done.slots_hbm = f32[4096,8,128]{2,1,0:T(8,128)} async-done(((f32[32,8,128]{2,1,0:T(8,128)}), f32[4096,8,128]{2,1,0:T(8,128)}) %all-gather.2.cloned.1.call-update) | async-done | bytes 16777232 | tf_op jit(solution)/shard_map/all_gather | solution.py:209
  102.3 27.0 %shard_map.61 = (f32[2048,1024]{1,0:T(8,128)}, f32[8,1024]{1,0:T(8,128)}) custom-call(s32[1024]{0:T(1024)} %get-tuple-element.7.idx_ref, s32[1]{0:T(128)} %bitcast.own_ref, f32[2048,1024]{1,0:T(8,128)} %shard_map.60.s_ref, f32[4096,8,128]{2,1,0:T(8,128)} %all-gather.2.cloned.1.call-done.slots_hbm, f32[8,128,128]{2,1,0:T(8,128)} %b_ref.3), custom_call_target="tpu_custom_call" | custom-call | tf_op jit(solution)/shard_map/pallas_call | solution.py:121
  (7 shorter events, 0.1 us)
Async XLA Ops:
  7.2 95.1 %all-gather.2.cloned.1.call-start = ((), (), s32[]{:S(2)}) async-start(), calls=%async_computation | async-start | bytes 16908288 | tf_op jit(solution)/shard_map/all_gather | solution.py:209
  16.0 2.5 %collective-permute-start = (f32[32,1024]{1,0:T(8,128)S(1)}, f32[32,1024]{1,0:T(8,128)S(1)}, u32[]{:S(2)}, u32[]{:S(2)}) collective-permute-start(f32[32,1024]{1,0:T(8,128)S(1)} %slice.9), channel_id=1, source_target_pairs={{0,1},{1,0},{2,3},{3,2},{4,5},{5,4},{6,7},{7,6},{8,9},{9,8},{10,11... | collective-permute-start | bytes 393224 | tf_op jit(solution)/shard_map/ppermute | solution.py:208
  19.3 10.6 %copy-start.1 = (bf16[1024,1024]{1,0:T(8,128)(2,1)S(1)}, bf16[1024,1024]{1,0:T(8,128)(2,1)}, u32[]{:S(2)}) copy-start(bf16[1024,1024]{1,0:T(8,128)(2,1)} %gauss_hbm.1) | copy-start | bytes 6291460
  29.8 6.5 %copy-start.2 = (bf16[2048,1024]{1,0:T(8,128)(2,1)S(1)}, bf16[2048,1024]{1,0:T(8,128)(2,1)}, u32[]{:S(2)}) copy-start(bf16[2048,1024]{1,0:T(8,128)(2,1)} %get-tuple-element.4) | copy-start | bytes 12582916
  29.9 6.5 %copy-start.3 = (bf16[1024,1024]{1,0:T(8,128)(2,1)S(1)}, bf16[1024,1024]{1,0:T(8,128)(2,1)}, u32[]{:S(2)}) copy-start(bf16[1024,1024]{1,0:T(8,128)(2,1)} %get-tuple-element.5) | copy-start | bytes 6291460
  36.3 6.8 %copy-start = (f32[8,128,128]{2,1,0:T(8,128)S(1)}, f32[8,128,128]{2,1,0:T(8,128)}, u32[]{:S(2)}) copy-start(f32[8,128,128]{2,1,0:T(8,128)} %b_ref.3) | copy-start | bytes 1572868
Sparse Core Ops, SparseCore 0:
  19.4 82.8 all-gather.1

commit v8 on v5

--- a/solution.py
+++ b/solution.py
@@ -79,7 +79,7 @@
             pltpu.make_async_copy(slots_hbm.at[pl.ds(idx_ref[r], 1)], pbuf.at[pl.ds(r, 1)], sem.at[0]).start()
             return carry
 
-        lax.fori_loop(0, used, fetch, 0, unroll=8)
+        lax.fori_loop(0, used, fetch, 0, unroll=32)
         first = own_ref[0] * share
         for r in range(share):
             pltpu.make_async_copy(slots_hbm.at[pl.ds(idx_ref[first + r], 1)], piv_ref.at[pl.ds(r, 1)], sem.at[1]).start()

time: 133 us -> 133 us (level)
  no operation moved by 1% of the time
where the time goes in v8:
time: 133 us; the launch traced here: 132 us
  waiting for transfers between devices  52.3 us (39%)
  Pallas kernels  41.5 us (31%)
  matrix products  19.2 us (14%)
  between operations  14.2 us (11%)
  other arithmetic  3.47 us (3%)
  starting transfers between devices  1.72 us (1%)
    all_gather x1, waiting for transfers between devices, on_device(): slots = lax.all_gather(own_slots, ('row', 'col'), tiled=True)  51.3 us
    pallas_call x1, Pallas kernels, solve(): pl.pallas_call(functools.partial(solve_kernel, 1.0 / k ** 0.5, share), ou...  23.1 us
    pallas_call x1, Pallas kernels, exchange(): pl.pallas_call(exchange_kernel, out_shape=(jax.ShapeDtypeStruct((rows, sl...  10.5 us
    pallas_call x1, Pallas kernels, scale(): pl.pallas_call(scale_kernel, out_shape=jax.ShapeDtypeStruct((rows, k), jn...  7.86 us
    dot_general x1, matrix products, on_device(): jnp.dot(other_slab, other_gauss, preferred_element_type=jnp.float32)  6.78 us
    dot_general x1, matrix products, on_device(): jnp.dot(mine, gauss, preferred_element_type=jnp.float32)  6.44 us
    dot_general x1, matrix products, on_device(): parts = jnp.dot(rows, gauss, preferred_element_type=jnp.float32)  5.96 us
  transfers between devices with their start and end apart: 2, of which 2 were waited for; matrix products, arithmetic and copies ran while one was open for 10% of the time, Pallas kernels for 14%

profile of v8, /device:TPU:1, one launch (start us, length us, event | category | flops | bytes accessed | tf_op | source)
XLA Modules:
  0.0 132.4 jit_solution(4452278855073453710)
XLA Ops:
  7.2 0.0 all-gather.2.cloned.1.call-start
  7.2 0.1 pad_add_fusion
  7.3 0.7 add_select_fusion
  8.0 0.5 convert_reduce_fusion
  8.5 1.3 multiply_subtract_fusion
  9.8 0.2 select_reduce_fusion
  10.1 6.0 %fusion.3 = f32[64,1024]{1,0:T(8,128)S(1)} fusion(bf16[1024,1024]{1,0:T(8,128)(2,1)} %gauss_hbm.1, bf16[4096,1024]{1,0:T(8,128)(2,1)} %slab_hbm.1, s32[64]{0:T(128)S(1)} %multiply_add_fusion.1), kind=kOutput, calls=%fused_computation.7 | convolution fusion | flops 671416320 | bytes 10748160 | tf_op jit(solution)/shard_map/dot_general | solution.py:205
  16.0 1.7 %collective-permute-start = (f32[32,1024]{1,0:T(8,128)S(1)}, f32[32,1024]{1,0:T(8,128)S(1)}, u32[]{:S(2)}, u32[]{:S(2)}) collective-permute-start(f32[32,1024]{1,0:T(8,128)S(1)} %slice.9), channel_id=1, source_target_pairs={{0,1},{1,0},{2,3},{3,2},{4,5},{5,4},{6,7},{7,6},{8,9},{9,8},{10,11... | collective-permute-start | bytes 393224 | tf_op jit(solution)/shard_map/ppermute | solution.py:206
  17.7 1.0 collective-permute-done
  18.7 0.7 slice_add_fusion
  19.4 0.0 all-gather.2.cloned.1.call-update
  19.4 0.0 copy-start.1
  19.4 10.5 %shard_map.59 = (bf16[2048,1024]{1,0:T(8,128)(2,1)}, bf16[1024,1024]{1,0:T(8,128)(2,1)}) custom-call(bf16[4096,1024]{1,0:T(8,128)(2,1)} %slab_hbm.1, bf16[1024,1024]{1,0:T(8,128)(2,1)} %gauss_hbm.1), custom_call_target="tpu_custom_call" | custom-call | tf_op jit(solution)/shard_map/pallas_call | solution.py:173
  30.0 0.0 copy-done.1
  30.0 0.0 copy-start.2
  30.0 0.0 copy-start.3
  30.0 6.4 %fusion = f32[2048,1024]{1,0:T(8,128)S(1)} fusion(bf16[1024,1024]{1,0:T(8,128)(2,1)S(1)} %copy-done.1, bf16[4096,1024]{1,0:T(8,128)(2,1)} %slab_hbm.1, s32[]{:T(128)S(6)} %select_n.13), kind=kOutput, calls=%fused_computation | convolution fusion | flops 4294967296 | bytes 14680068 | tf_op jit(solution)/shard_map/dot_general | solution.py:211
  36.5 0.0 copy-done.2
  36.5 0.0 copy-done.3
  36.5 0.0 copy-start
  36.5 6.8 %convolution_add_fusion.s_ref = f32[2048,1024]{1,0:T(8,128)} fusion(f32[2048,1024]{1,0:T(8,128)S(1)} %fusion, bf16[2048,1024]{1,0:T(8,128)(2,1)S(1)} %copy-done.2, bf16[1024,1024]{1,0:T(8,128)(2,1)S(1)} %copy-done.3), kind=kOutput, calls=%fused_computation.5 | convolution fusion | flops 4297064448 | bytes 23068672 | tf_op jit(solution)/shard_map/dot_general | solution.py:211
  43.3 0.0 copy-done
  43.3 7.9 %shard_map.60.s_ref = f32[2048,1024]{1,0:T(8,128)} custom-call(f32[2048,1024]{1,0:T(8,128)} %convolution_add_fusion.s_ref, f32[8,128,128]{2,1,0:T(8,128)S(1)} %copy-done), custom_call_target="tpu_custom_call" | custom-call | tf_op jit(solution)/shard_map/pallas_call | solution.py:58
  51.1 51.3 %all-gather.2.cloned.1.call-done.slots_hbm = f32[4096,1024]{1,0:T(8,128)} async-done(((f32[32,1024]{1,0:T(8,128)}), f32[4096,1024]{1,0:T(8,128)}) %all-gather.2.cloned.1.call-update) | async-done | bytes 16777232 | tf_op jit(solution)/shard_map/all_gather | solution.py:207
  102.5 23.1 %shard_map.61 = (f32[2048,1024]{1,0:T(8,128)}, f32[8,1024]{1,0:T(8,128)}) custom-call(s32[1024]{0:T(1024)} %get-tuple-element.7.idx_ref, s32[1]{0:T(128)} %bitcast.own_ref, f32[2048,1024]{1,0:T(8,128)} %shard_map.60.s_ref, f32[4096,1024]{1,0:T(8,128)} %all-gather.2.cloned.1.call-done.slots_hbm, f32[8,128,128]{2,1,0:T(8,128)} %b_ref.3), custom_call_target="tpu_custom_call" | custom-call | tf_op jit(solution)/shard_map/pallas_call | solution.py:120
  (6 shorter events, 0.0 us)
Async XLA Ops:
  7.2 95.3 %all-gather.2.cloned.1.call-start = ((), (), s32[]{:S(2)}) async-start(), calls=%async_computation | async-start | bytes 16908288 | tf_op jit(solution)/shard_map/all_gather | solution.py:207
  16.0 2.7 %collective-permute-start = (f32[32,1024]{1,0:T(8,128)S(1)}, f32[32,1024]{1,0:T(8,128)S(1)}, u32[]{:S(2)}, u32[]{:S(2)}) collective-permute-start(f32[32,1024]{1,0:T(8,128)S(1)} %slice.9), channel_id=1, source_target_pairs={{0,1},{1,0},{2,3},{3,2},{4,5},{5,4},{6,7},{7,6},{8,9},{9,8},{10,11... | collective-permute-start | bytes 393224 | tf_op jit(solution)/shard_map/ppermute | solution.py:206
  19.4 10.6 %copy-start.1 = (bf16[1024,1024]{1,0:T(8,128)(2,1)S(1)}, bf16[1024,1024]{1,0:T(8,128)(2,1)}, u32[]{:S(2)}) copy-start(bf16[1024,1024]{1,0:T(8,128)(2,1)} %gauss_hbm.1) | copy-start | bytes 6291460
  30.0 6.5 %copy-start.2 = (bf16[2048,1024]{1,0:T(8,128)(2,1)S(1)}, bf16[2048,1024]{1,0:T(8,128)(2,1)}, u32[]{:S(2)}) copy-start(bf16[2048,1024]{1,0:T(8,128)(2,1)} %get-tuple-element.4) | copy-start | bytes 12582916
  30.0 6.5 %copy-start.3 = (bf16[1024,1024]{1,0:T(8,128)(2,1)S(1)}, bf16[1024,1024]{1,0:T(8,128)(2,1)}, u32[]{:S(2)}) copy-start(bf16[1024,1024]{1,0:T(8,128)(2,1)} %get-tuple-element.5) | copy-start | bytes 6291460
  36.5 6.8 %copy-start = (f32[8,128,128]{2,1,0:T(8,128)S(1)}, f32[8,128,128]{2,1,0:T(8,128)}, u32[]{:S(2)}) copy-start(f32[8,128,128]{2,1,0:T(8,128)} %b_ref.3) | copy-start | bytes 1572868
Sparse Core Ops, SparseCore 0:
  19.5 82.8 all-gather.1

commit v9 on v8

--- a/solution.py
+++ b/solution.py
@@ -198,7 +198,11 @@
     targets = jnp.concatenate([jnp.full((SLOTS,), owner), jnp.full((SLOTS,), partner)])
     offsets = jnp.concatenate([jnp.full((SLOTS,), col), jnp.full((SLOTS,), 1 - col)]) * shard_rows
     slot_ids = jnp.concatenate([jnp.arange(SLOTS), jnp.arange(SLOTS)])
-    hit = (block_of[None, :] == targets[:, None]) & (rank[None, :] == slot_ids[:, None])
+    in_target = (block_of[None, :] == jnp.stack([owner, partner])[:, None]).astype(jnp.bfloat16)
+    before = (order[:, None] < order[None, :]).astype(jnp.bfloat16)
+    count = jnp.dot(in_target, before, preferred_element_type=jnp.float32).astype(jnp.int32)
+    counts = jnp.concatenate([jnp.broadcast_to(count[0], (SLOTS, count.shape[1])), jnp.broadcast_to(count[1], (SLOTS, count.shape[1]))])
+    hit = (block_of[None, :] == targets[:, None]) & (counts == slot_ids[:, None])
     where_row = jnp.sum(jnp.where(hit, local[None, :], 0), axis=1) + offsets
     pick = where_row[:, None] == jnp.arange(slab.shape[0], dtype=jnp.int32)[None, :]
     rows = jnp.dot(pick.astype(slab.dtype), slab, preferred_element_type=jnp.float32).astype(slab.dtype)

time: 133 us -> 133 us (level)
  no operation moved by 1% of the time
where the time goes in v9:
time: 133 us
  waiting for transfers between devices  52.3 us (39%)
  Pallas kernels  41.5 us (31%)
  matrix products  19.5 us (15%)
  between operations  14.2 us (11%)
  other arithmetic  3.53 us (3%)
  starting transfers between devices  1.72 us (1%)
    all_gather x1, waiting for transfers between devices, on_device(): slots = lax.all_gather(own_slots, ('row', 'col'), tiled=True)  51.3 us
    pallas_call x1, Pallas kernels, solve(): pl.pallas_call(functools.partial(solve_kernel, 1.0 / k ** 0.5, share), ou...  23.1 us
    pallas_call x1, Pallas kernels, exchange(): pl.pallas_call(exchange_kernel, out_shape=(jax.ShapeDtypeStruct((rows, sl...  10.5 us
    pallas_call x1, Pallas kernels, scale(): pl.pallas_call(scale_kernel, out_shape=jax.ShapeDtypeStruct((rows, k), jn...  7.87 us
    dot_general x1, matrix products, on_device(): jnp.dot(other_slab, other_gauss, preferred_element_type=jnp.float32)  6.78 us
    dot_general x1, matrix products, on_device(): jnp.dot(mine, gauss, preferred_element_type=jnp.float32)  6.44 us
    dot_general x1, matrix products, on_device(): parts = jnp.dot(rows, gauss, preferred_element_type=jnp.float32)  5.96 us
  transfers between devices with their start and end apart: 2, of which 2 were waited for; matrix products, arithmetic and copies ran while one was open for 10% of the time, Pallas kernels for 14%

profile of v9, /device:TPU:1, one launch (start us, length us, event | category | flops | bytes accessed | tf_op | source)
XLA Modules:
  0.0 132.9 jit_solution(7847882946524273346)
XLA Ops:
  7.2 0.0 all-gather.2.cloned.1.call-start
  7.2 0.1 pad_add_fusion.1
  7.3 0.7 add_select_fusion
  8.0 0.5 convert_reduce_fusion
  8.5 1.3 multiply_subtract_fusion
  9.8 0.1 pad_add_fusion
  9.9 0.4 fusion.4
  10.3 0.2 select_reduce_fusion
  10.5 6.0 %fusion.5 = f32[64,1024]{1,0:T(8,128)S(1)} fusion(bf16[1024,1024]{1,0:T(8,128)(2,1)} %gauss_hbm.1, bf16[4096,1024]{1,0:T(8,128)(2,1)} %slab_hbm.1, s32[64]{0:T(128)S(1)} %multiply_add_fusion.1), kind=kOutput, calls=%fused_computation.10 | convolution fusion | flops 671416320 | bytes 10748160 | tf_op jit(solution)/shard_map/dot_general | solution.py:209
  16.5 1.7 %collective-permute-start = (f32[32,1024]{1,0:T(8,128)S(1)}, f32[32,1024]{1,0:T(8,128)S(1)}, u32[]{:S(2)}, u32[]{:S(2)}) collective-permute-start(f32[32,1024]{1,0:T(8,128)S(1)} %slice.19), channel_id=1, source_target_pairs={{0,1},{1,0},{2,3},{3,2},{4,5},{5,4},{6,7},{7,6},{8,9},{9,8},{10,11... | collective-permute-start | bytes 393224 | tf_op jit(solution)/shard_map/ppermute | solution.py:210
  18.2 1.0 collective-permute-done
  19.2 0.7 slice_add_fusion
  19.9 0.0 all-gather.2.cloned.1.call-update
  19.9 0.0 copy-start.1
  19.9 10.5 %shard_map.59 = (bf16[2048,1024]{1,0:T(8,128)(2,1)}, bf16[1024,1024]{1,0:T(8,128)(2,1)}) custom-call(bf16[4096,1024]{1,0:T(8,128)(2,1)} %slab_hbm.1, bf16[1024,1024]{1,0:T(8,128)(2,1)} %gauss_hbm.1), custom_call_target="tpu_custom_call" | custom-call | tf_op jit(solution)/shard_map/pallas_call | solution.py:173
  30.5 0.0 copy-done.1
  30.5 0.0 copy-start.2
  30.5 0.0 copy-start.3
  30.5 6.4 %fusion = f32[2048,1024]{1,0:T(8,128)S(1)} fusion(bf16[1024,1024]{1,0:T(8,128)(2,1)S(1)} %copy-done.1, bf16[4096,1024]{1,0:T(8,128)(2,1)} %slab_hbm.1, s32[]{:T(128)S(6)} %select_n.13), kind=kOutput, calls=%fused_computation.1 | convolution fusion | flops 4294967296 | bytes 14680068 | tf_op jit(solution)/shard_map/dot_general | solution.py:215
  36.9 0.0 copy-done.2
  36.9 0.0 copy-done.3
  37.0 0.0 copy-start
  37.0 6.8 %convolution_add_fusion.s_ref = f32[2048,1024]{1,0:T(8,128)} fusion(f32[2048,1024]{1,0:T(8,128)S(1)} %fusion, bf16[2048,1024]{1,0:T(8,128)(2,1)S(1)} %copy-done.2, bf16[1024,1024]{1,0:T(8,128)(2,1)S(1)} %copy-done.3), kind=kOutput, calls=%fused_computation.7 | convolution fusion | flops 4297064448 | bytes 23068672 | tf_op jit(solution)/shard_map/dot_general | solution.py:215
  43.8 0.0 copy-done
  43.8 7.9 %shard_map.60.s_ref = f32[2048,1024]{1,0:T(8,128)} custom-call(f32[2048,1024]{1,0:T(8,128)} %convolution_add_fusion.s_ref, f32[8,128,128]{2,1,0:T(8,128)S(1)} %copy-done), custom_call_target="tpu_custom_call" | custom-call | tf_op jit(solution)/shard_map/pallas_call | solution.py:58
  51.6 51.3 %all-gather.2.cloned.1.call-done.slots_hbm = f32[4096,1024]{1,0:T(8,128)} async-done(((f32[32,1024]{1,0:T(8,128)}), f32[4096,1024]{1,0:T(8,128)}) %all-gather.2.cloned.1.call-update) | async-done | bytes 16777232 | tf_op jit(solution)/shard_map/all_gather | solution.py:211
  102.9 23.1 %shard_map.61 = (f32[2048,1024]{1,0:T(8,128)}, f32[8,1024]{1,0:T(8,128)}) custom-call(s32[1024]{0:T(1024)} %get-tuple-element.9.idx_ref, s32[1]{0:T(128)} %bitcast.own_ref, f32[2048,1024]{1,0:T(8,128)} %shard_map.60.s_ref, f32[4096,1024]{1,0:T(8,128)} %all-gather.2.cloned.1.call-done.slots_hbm, f32[8,128,128]{2,1,0:T(8,128)} %b_ref.3), custom_call_target="tpu_custom_call" | custom-call | tf_op jit(solution)/shard_map/pallas_call | solution.py:120
  (9 shorter events, 0.1 us)
Async XLA Ops:
  7.2 95.8 %all-gather.2.cloned.1.call-start = ((), (), s32[]{:S(2)}) async-start(), calls=%async_computation | async-start | bytes 16908288 | tf_op jit(solution)/shard_map/all_gather | solution.py:211
  16.5 2.7 %collective-permute-start = (f32[32,1024]{1,0:T(8,128)S(1)}, f32[32,1024]{1,0:T(8,128)S(1)}, u32[]{:S(2)}, u32[]{:S(2)}) collective-permute-start(f32[32,1024]{1,0:T(8,128)S(1)} %slice.19), channel_id=1, source_target_pairs={{0,1},{1,0},{2,3},{3,2},{4,5},{5,4},{6,7},{7,6},{8,9},{9,8},{10,11... | collective-permute-start | bytes 393224 | tf_op jit(solution)/shard_map/ppermute | solution.py:210
  19.9 10.6 %copy-start.1 = (bf16[1024,1024]{1,0:T(8,128)(2,1)S(1)}, bf16[1024,1024]{1,0:T(8,128)(2,1)}, u32[]{:S(2)}) copy-start(bf16[1024,1024]{1,0:T(8,128)(2,1)} %gauss_hbm.1) | copy-start | bytes 6291460
  30.5 6.5 %copy-start.2 = (bf16[2048,1024]{1,0:T(8,128)(2,1)S(1)}, bf16[2048,1024]{1,0:T(8,128)(2,1)}, u32[]{:S(2)}) copy-start(bf16[2048,1024]{1,0:T(8,128)(2,1)} %get-tuple-element.4) | copy-start | bytes 12582916
  30.5 6.5 %copy-start.3 = (bf16[1024,1024]{1,0:T(8,128)(2,1)S(1)}, bf16[1024,1024]{1,0:T(8,128)(2,1)}, u32[]{:S(2)}) copy-start(bf16[1024,1024]{1,0:T(8,128)(2,1)} %get-tuple-element.5) | copy-start | bytes 6291460
  37.0 6.8 %copy-start = (f32[8,128,128]{2,1,0:T(8,128)S(1)}, f32[8,128,128]{2,1,0:T(8,128)}, u32[]{:S(2)}) copy-start(f32[8,128,128]{2,1,0:T(8,128)} %b_ref.3) | copy-start | bytes 1572868
Sparse Core Ops, SparseCore 0:
  20.0 82.8 all-gather.1
